TPU v7x, 128 devices: a whole 4x4x4 slice. The times are simulated.
128 devices in a mesh: lon: 32 (over y, z, core), lat: 4 (over x).
Axes of the slice: x: 4, y: 4, z: 4, core: 2. Of those that a mesh axis runs over, the one named last changes fastest.
Arguments:
- spectrum: float32 [36, 36, 128, 512], P(None, None, 'lon', 'lat'), may hold values from 0.05 to 2
- sea_mask: int32 [128, 512], P('lon', 'lat'), may hold values 0 or 1
- refraction: float32 [2, 128, 512], P(None, 'lon', 'lat'), may hold values from -0.35 to 0.35
- atm_wind: float32 [2, 2, 16384], P(None, None, ('lon', 'lat')), may hold values from -20 to 20
- hour_fraction: float32 [1], replicated, may hold values from 0 to 1
- send_cells: int32 [128, 192], P(('lon', 'lat')), may hold values from 0 to 127, as said below
- recv_slots: int32 [4, 128, 512], P(None, 'lon', 'lat'), may hold values from 0 to 191, as said below
- recv_weights: float32 [4, 128, 512], P(None, 'lon', 'lat'), may hold values from 0.05 to 0.45
Outputs:
- spectrum_next: float32 [36, 36, 128, 512], P(None, None, 'lon', 'lat')
- surface_wind: float32 [2, 128, 512], P(None, 'lon', 'lat')
Inputs may be any that keep to these rules, and one draw needn't show every extreme that they name: `send_cells`: row t holds, for each of the 32 wave tiles of tile t's latitude band in lon order, a block of 6 local atmosphere cells of tile t; every entry is read by some wave cell. `recv_slots`: entry e of a wave cell refers to position e % 6 of the block that the atmosphere tile at lon index e // 6 of the same latitude band lists for this cell's wave tile.
All inputs are finite; a program needn't handle non-finite values. No bound on the sum of `sea_mask` on one device may be relied on, other than what follows from the above.
Results may differ from a plain program's by a relative error of at most 0.0003.
Values sent between devices are 32-bit elements; how exact they have to be, the bound alone decides.
A program may use at most 128 MiB of HBM per device.

v0:
```python
import math

import jax
import jax.numpy as jnp
from jax import lax
from jax.sharding import PartitionSpec as P

base_freq = 0.035
freq_step = 1.1
courant_max = 0.9
gravity = 9.81
input_rate = 0.05
damping_rate = 0.8
energy_ref = 0.5


def padded_2(value, sides, width, wrap):
    for axis, dim in sides:
        size, length = (lax.axis_size(axis), value.shape[dim])
        up = [(i, (i + 1) % size) for i in range(size if wrap else size - 1)]
        down = [(j, i) for i, j in up]
        last = lax.slice_in_dim(value, length - width, length, axis=dim)
        initial = lax.slice_in_dim(value, 0, width, axis=dim)
        before = lax.ppermute(last, axis, up)
        after = lax.ppermute(initial, axis, down)
        value = jnp.concatenate([before, value, after], axis=dim)
    return value


def spectral_tables(freq_count, dir_count):
    frequencies = base_freq * freq_step ** jnp.arange(freq_count, dtype=jnp.float32)
    spacing = 2.0 * math.pi / dir_count
    angles = (jnp.arange(dir_count, dtype=jnp.float32) + 0.5) * spacing
    face_angles = (jnp.arange(dir_count, dtype=jnp.float32) + 1.0) * spacing
    return (frequencies, angles, face_angles)


def transport(padded, courant, dimension):
    length = padded.shape[dimension] - 4
    far_left = lax.slice_in_dim(padded, 0, length + 1, axis=dimension)
    left_cell = lax.slice_in_dim(padded, 1, length + 2, axis=dimension)
    right_cell = lax.slice_in_dim(padded, 2, length + 3, axis=dimension)
    far_right = lax.slice_in_dim(padded, 3, length + 4, axis=dimension)
    forward = courant > 0
    upwind = jnp.where(forward, left_cell, right_cell)
    downwind = jnp.where(forward, right_cell, left_cell)
    beyond = jnp.where(forward, far_left, far_right)
    magnitude = jnp.abs(courant)
    face_flux = courant * (
        upwind
        + 0.5 * (1.0 - magnitude) * (downwind - upwind)
        - (1.0 - magnitude * magnitude) / 6.0 * (downwind - 2.0 * upwind + beyond)
    )
    return lax.slice_in_dim(face_flux, 1, length + 1, axis=dimension) - lax.slice_in_dim(
        face_flux, 0, length, axis=dimension
    )


def local(
    spectrum, sea_mask, refraction, atm_wind, hour_fraction, send_cells, recv_slots, recv_weights
):
    freq_count = spectrum.shape[0]
    dir_count = spectrum.shape[1]
    sea_frac = sea_mask.astype(jnp.float32)
    frequencies, angles, face_angles = spectral_tables(freq_count, dir_count)
    period_ratio = base_freq / frequencies
    courant_lon = (courant_max * period_ratio[:, None] * jnp.cos(angles)[None, :])[:, :, None, None]
    courant_lat = (courant_max * period_ratio[:, None] * jnp.sin(angles)[None, :])[:, :, None, None]
    bending = jnp.sqrt(period_ratio)
    face_sin = jnp.sin(face_angles)[:, None, None]
    face_cos = jnp.cos(face_angles)[:, None, None]
    weight_late = hour_fraction[0]
    wind_now = (1.0 - weight_late) * atm_wind[0] + weight_late * atm_wind[1]
    packed = wind_now[:, send_cells[0]]
    received = lax.all_to_all(packed, "lon", split_axis=1, concat_axis=1, tiled=True)
    picked = received[:, recv_slots]
    surface_wind = jnp.sum(recv_weights[None] * picked, axis=1)
    density = spectrum
    padded = padded_2(density, (("lon", 2),), 2, True)
    density = (density - transport(padded, courant_lon, 2)) * sea_frac
    padded = padded_2(density, (("lat", 3),), 2, False)
    density = (density - transport(padded, courant_lat, 3)) * sea_frac
    face_speed = bending[:, None, None, None] * (
        refraction[0][None, None] * face_sin[None] - refraction[1][None, None] * face_cos[None]
    )
    next_dir = jnp.roll(density, -1, axis=1)
    face_flux = jnp.maximum(face_speed, 0.0) * density + jnp.minimum(face_speed, 0.0) * next_dir
    refracted = density - (face_flux - jnp.roll(face_flux, 1, axis=1))
    energy = jnp.mean(refracted, axis=(0, 1))
    energy_ratio = energy / energy_ref
    damping = energy_ratio * energy_ratio
    projected = (
        surface_wind[0][None] * jnp.cos(angles)[:, None, None]
        + surface_wind[1][None] * jnp.sin(angles)[:, None, None]
    )
    rel_freq = (frequencies / frequencies[freq_count - 1])[:, None, None, None]
    slowness = (2.0 * math.pi * frequencies / gravity)[:, None, None, None]
    growth = input_rate * rel_freq * jnp.maximum(projected[None] * slowness - 1.0, 0.0)
    decay_rate = damping_rate * rel_freq * damping[None, None]
    spectrum_next = refracted * jnp.exp(growth - decay_rate)
    return (spectrum_next, surface_wind)


def solution(mesh):
    in_specs = (
        P(None, None, "lon", "lat"),
        P("lon", "lat"),
        P(None, "lon", "lat"),
        P(None, None, ("lon", "lat")),
        P(),
        P(("lon", "lat"), None),
        P(None, "lon", "lat"),
        P(None, "lon", "lat"),
    )
    out_specs = (P(None, None, "lon", "lat"), P(None, "lon", "lat"))
    return jax.shard_map(local, mesh=mesh, in_specs=in_specs, out_specs=out_specs, check_vma=False)
```

profile of v0, /device:TPU:0, one launch (start us, length us, event | category | flops | bytes accessed | tf_op | source)
XLA Modules:
  0.0 199.4 jit_solution(16966382026487158103)
XLA Ops:
  0.6 0.0 copy-start.1
  0.6 0.0 copy-start.5
  0.7 0.0 copy-start.7
  0.7 0.0 copy-start.4
  0.7 0.0 copy-start.3
  0.7 3.8 %fusion.40 = (f32[36,36,2,128]{3,2,1,0:T(2,128)S(1)}, f32[36,36,2,128]{3,2,1,0:T(2,128)S(1)}) fusion(f32[36,36,4,128]{3,2,1,0:T(4,128)} %param.8), kind=kLoop, calls=%fused_computation.89 | loop fusion | bytes 5308416 | tf_op jit(solution)/shard_map/slice | solution.py:22
  4.5 0.0 copy-start.6
  4.5 0.0 copy-start.2
  4.5 1.2 copy.111
  5.8 6.0 %collective-permute-start.1 = (f32[36,36,2,128]{3,1,2,0:T(8,128)}, f32[36,36,2,128]{3,1,2,0:T(8,128)}, u32[]{:S(2)}, u32[]{:S(2)}) collective-permute-start(f32[36,36,2,128]{3,1,2,0:T(8,128)} %copy.111), channel_id=1, source_target_pairs={{4,0},{8,4},{12,8},{16,12},{20,16},{24,20},{28,24},{32,28},{36,32}... | collective-permute-start | bytes 3981320 | tf_op jit(solution)/shard_map/ppermute | solution.py:25
  11.8 1.2 copy.110
  13.0 0.0 collective-permute-start
  13.7 0.0 copy-done.5
  13.7 0.1 copy.103
  13.8 0.0 copy-done.7
  13.8 0.7 gather_fusion
  14.5 0.1 copy.104
  14.6 0.1 all_to_all.8
  14.7 0.6 copy.105
  15.4 6.7 %all-to-all-start = ((f32[2,32,6]{2,0,1:T(2,128)}), f32[2,32,6]{2,0,1:T(2,128)S(1)}, u32[]{:S(2)}, u32[]{:S(2)}) async-start(f32[2,32,6]{2,0,1:T(2,128)} %copy.105), calls=%async_computation | async-start | bytes 65536 | tf_op jit(solution)/shard_map/all_to_all | solution.py:75
  22.2 0.1 fusion.34
  22.3 0.0 copy-done.4
  22.3 0.6 slice.115
  22.9 0.7 broadcast_multiply_fusion.3
  23.5 0.1 multiply_compare_fusion
  23.6 0.0 copy-done.3
  23.6 0.1 broadcast_multiply_fusion.1
  23.7 0.2 multiply_subtract_fusion
  24.0 0.0 copy-done.1
  24.0 6.9 %copy.102 = f32[36,36,4,128]{1,0,3,2:T(8,128)} copy(f32[36,36,4,128]{3,2,1,0:T(4,128)S(1)} %copy-done.1) | data formatting | bytes 5308416 | tf_op args[0]
  30.9 0.0 copy-done.6
  30.9 4.9 %all-to-all-done = f32[2,32,6]{2,0,1:T(2,128)S(1)} async-done(((f32[2,32,6]{2,0,1:T(2,128)}), f32[2,32,6]{2,0,1:T(2,128)S(1)}, u32[]{:S(2)}, u32[]{:S(2)}) %all-to-all-start) | async-done | bytes 1568 | tf_op jit(solution)/shard_map/all_to_all | solution.py:75
  35.8 0.1 all_to_all.10
  35.9 0.1 copy.107
  36.0 5.5 %gather_fusion.1 = f32[2048,2]{1,0:T(8,128)S(1)} fusion(f32[2,192]{0,1:T(8,128)S(1)} %copy.107, s32[2048]{0:T(1024)S(1)} %broadcast_clamp_fusion), kind=kCustom, calls=%fused_computation.1 | custom fusion | bytes 40960 | tf_op jit(solution)/shard_map/gather | solution.py:76
  41.5 0.0 copy-done.2
  41.5 0.3 multiply_reduce_fusion
  41.9 0.3 slice_reduce_fusion.1
  42.2 0.0 collective-permute-done.1
  42.2 5.2 %copy.101 = f32[36,36,2,128]{1,0,3,2:T(8,128)} copy(f32[36,36,2,128]{3,1,2,0:T(8,128)} %collective-permute-done.1) | data formatting | bytes 2654208 | tf_op jit(solution)/shard_map/ppermute | solution.py:25
  47.4 0.0 collective-permute-done
  47.4 5.0 %copy.97 = f32[36,36,2,128]{1,0,3,2:T(8,128)} copy(f32[36,36,2,128]{3,1,2,0:T(8,128)} %collective-permute-done) | data formatting | bytes 2654208 | tf_op jit(solution)/shard_map/ppermute | solution.py:24
  52.4 23.2 %fusion.6 = f32[36,36,5,128]{1,0,3,2:T(8,128)} fusion(f32[36,36,2,128]{1,0,3,2:T(8,128)} %copy.101, f32[36,36,4,128]{1,0,3,2:T(8,128)} %copy.102, f32[36,36,2,128]{1,0,3,2:T(8,128)} %copy.97, f32[36,36]{1,0:T(8,128)S(1)} %get-tuple-element.31, f32[36,36]{1,0:T(8,128)S(1)} %get-tuple-element.30, f32[36,36]{1,0:T(8,128)S(1)} %get-tuple-element.32, ...), kind=kLoop, calls=%fused_computation.15 | loop fusion | flops 13271040 | bytes 8643024 | tf_op jit(solution)/shard_map/mul | solution.py:49
  75.7 10.8 %fusion.20 = f32[36,36,4,128]{1,0,3,2:T(8,128)S(1)} fusion(f32[36,36,4,128]{1,0,3,2:T(8,128)} %copy.102, f32[36,36,5,128]{1,0,3,2:T(8,128)} %fusion.6, f32[4,128]{1,0:T(4,128)S(1)} %convert_element_type.3), kind=kLoop, calls=%fused_computation.38 | loop fusion | flops 1990656 | bytes 10618880 | tf_op jit(solution)/shard_map/mul | solution.py:80
  86.5 0.0 copy-start
  86.5 3.8 %copy-done = f32[36,36,4,128]{1,0,3,2:T(8,128)} copy-done((f32[36,36,4,128]{1,0,3,2:T(8,128)}, f32[36,36,4,128]{1,0,3,2:T(8,128)S(1)}, u32[]{:S(2)}) %copy-start) | copy-done | bytes 2654232
  90.4 3.4 %collective-permute-start.2 = (f32[36,36,4,2]{1,0,3,2:T(8,128)S(1)}, f32[36,36,4,2]{1,0,3,2:T(8,128)S(1)}, u32[]{:S(2)}, u32[]{:S(2)}) collective-permute-start(f32[36,36,4,2]{1,0,3,2:T(8,128)S(1)} %get-tuple-element.16), channel_id=1, source_target_pairs={{0,1},{1,2},{2,3},{4,5},{5,6},{6,7},{8,9},{9,10},{10,11},{12,13},{... | collective-permute-start | bytes 124424 | tf_op jit(solution)/shard_map/ppermute | solution.py:24
  93.8 1.3 collective-permute-start.3
  95.1 0.2 multiply_add_fusion
  95.3 0.7 copy.109
  96.0 1.5 collective-permute-done.2
  97.5 4.1 %collective-permute-done.3 = f32[36,36,4,2]{1,0,3,2:T(8,128)S(1)} collective-permute-done((f32[36,36,4,2]{1,0,3,2:T(8,128)S(1)}, f32[36,36,4,2]{1,0,3,2:T(8,128)S(1)}, u32[]{:S(2)}, u32[]{:S(2)}) %collective-permute-start.3) | collective-permute-done | bytes 41504 | tf_op jit(solution)/shard_map/ppermute | solution.py:25
  101.6 21.1 %fusion.13 = f32[36,36,4,129]{1,0,3,2:T(8,128)} fusion(f32[36,36,4,2]{1,0,3,2:T(8,128)S(1)} %collective-permute-done.3, f32[36,36,4,128]{1,0,3,2:T(8,128)} %copy-done, f32[36,36,4,2]{1,0,3,2:T(8,128)S(1)} %collective-permute-done.2, f32[36,36]{1,0:T(8,128)S(1)} %get-tuple-element.23, f32[36,36]{1,0:T(8,128)S(1)} %get-tuple-element.24, ...), kind=kLoop, calls=%fused_computation.28 | loop fusion | flops 10699776 | bytes 5428944 | tf_op jit(solution)/shard_map/mul | solution.py:49
  122.7 10.9 %fusion.18 = f32[36,36,4,128]{1,0,3,2:T(8,128)S(1)} fusion(f32[36,36,4,128]{1,0,3,2:T(8,128)} %copy-done, f32[36,36,4,129]{1,0,3,2:T(8,128)} %fusion.13, f32[4,128]{1,0:T(4,128)S(1)} %convert_element_type.3), kind=kLoop, calls=%fused_computation.35 | loop fusion | flops 1990656 | bytes 10618880 | tf_op jit(solution)/shard_map/mul | solution.py:82
  133.6 6.6 %slice.138 = f32[36,35,4,128]{1,0,3,2:T(8,128)} slice(f32[36,36,4,128]{1,0,3,2:T(8,128)S(1)} %fusion.18), slice={[0:36], [1:36], [0:4], [0:128]} | slice | bytes 5160960 | tf_op jit(solution)/shard_map/jit(_roll_static)/slice | solution.py:86
  140.2 10.9 %fusion.15 = f32[36,36,4,128]{1,0,3,2:T(8,128)} fusion(f32[36,36,4,128]{1,0,3,2:T(8,128)S(1)} %fusion.18, f32[36,1,4,128]{1,0,3,2:T(8,128)S(1)} %bitcast.19, f32[36,35,4,128]{1,0,3,2:T(8,128)} %slice.138, f32[36,4,128]{0,2,1:T(8,128)S(1)} %multiply_subtract_fusion, f32[36]{0:T(128)S(1)} %fusion.36), kind=kLoop, calls=%fused_computation.31 | loop fusion | flops 4644864 | bytes 8036496 | tf_op jit(solution)/shard_map/add | solution.py:87
  151.1 10.6 %slice.140 = f32[36,1,4,128]{1,0,3,2:T(8,128)} slice(f32[36,36,4,128]{1,0,3,2:T(8,128)} %fusion.15), slice={[0:36], [35:36], [0:4], [0:128]} | slice | bytes 147456 | tf_op jit(solution)/shard_map/jit(_roll_static)/slice | solution.py:88
  161.7 18.3 %fusion.37 = (f32[4,128]{1,0:T(4,128)S(1)}, f32[36,36,4,128]{1,0,3,2:T(8,128)}) fusion(f32[36,36,4,128]{1,0,3,2:T(8,128)S(1)} %fusion.18, f32[36,36,4,128]{1,0,3,2:T(8,128)} %fusion.15, f32[36,35,4,128]{1,0,3,2:T(8,128)} %bitcast.20, f32[36,1,4,128]{1,0,3,2:T(8,128)} %slice.140), kind=kLoop, calls=%fused_computation.87 | loop fusion | flops 2653696 | bytes 10618880 | tf_op jit(solution)/shard_map/reduce_sum | solution.py:89
  179.9 0.1 broadcast_multiply_fusion
  180.1 11.1 %exponential_multiply_fusion = f32[36,36,4,128]{1,0,3,2:T(8,128)} fusion(f32[36,36,4,128]{1,0,3,2:T(8,128)} %get-tuple-element.15, f32[36,4,128]{0,2,1:T(8,128)S(1)} %broadcast_multiply_fusion, f32[36]{0:T(128)S(1)} %fusion.30, f32[36,4,128]{0,2,1:T(8,128)S(1)} %multiply_add_fusion, f32[36]{0:T(128)S(1)} %get-tuple-element.38), kind=kLoop, calls=%fused_computation.41 | loop fusion | flops 3981312 | bytes 5456160 | tf_op jit(solution)/shard_map/mul | solution.py:100
  191.1 8.3 %copy.108 = f32[36,36,4,128]{3,2,1,0:T(4,128)} copy(f32[36,36,4,128]{1,0,3,2:T(8,128)} %exponential_multiply_fusion) | data formatting | bytes 5308416
  (15 shorter events, 0.2 us)
Async XLA Ops:
  0.6 23.3 %copy-start.1 = (f32[36,36,4,128]{3,2,1,0:T(4,128)S(1)}, f32[36,36,4,128]{3,2,1,0:T(4,128)}, u32[]{:S(2)}) copy-start(f32[36,36,4,128]{3,2,1,0:T(4,128)} %param.8) | copy-start | bytes 7962628
  0.6 13.0 %copy-start.5 = (f32[2,2,128]{2,1,0:T(2,128)S(1)}, f32[2,2,128]{2,1,0:T(2,128)}, u32[]{:S(2)}) copy-start(f32[2,2,128]{2,1,0:T(2,128)} %param.11) | copy-start | bytes 6148
  0.7 13.2 %copy-start.7 = (s32[1,192]{1,0:T(1,128)S(1)}, s32[1,192]{1,0:T(1,128)}, u32[]{:S(2)}) copy-start(s32[1,192]{1,0:T(1,128)} %param.13) | copy-start | bytes 2308
  0.7 21.6 %copy-start.4 = (f32[2,4,128]{2,1,0:T(4,128)S(1)}, f32[2,4,128]{2,1,0:T(4,128)}, u32[]{:S(2)}) copy-start(f32[2,4,128]{2,1,0:T(4,128)} %param.10) | copy-start | bytes 12292
  0.7 22.9 %copy-start.3 = (s32[4,4,128]{2,1,0:T(4,128)S(1)}, s32[4,4,128]{2,1,0:T(4,128)}, u32[]{:S(2)}) copy-start(s32[4,4,128]{2,1,0:T(4,128)} %param.14) | copy-start | bytes 24580
  4.5 26.4 %copy-start.6 = (s32[4,128]{1,0:T(4,128)S(1)}, s32[4,128]{1,0:T(4,128)}, u32[]{:S(2)}) copy-start(s32[4,128]{1,0:T(4,128)} %param.9) | copy-start | bytes 6148
  4.5 37.0 %copy-start.2 = (f32[4,4,128]{2,1,0:T(4,128)S(1)}, f32[4,4,128]{2,1,0:T(4,128)}, u32[]{:S(2)}) copy-start(f32[4,4,128]{2,1,0:T(4,128)} %param.15) | copy-start | bytes 24580
  5.8 36.4 %collective-permute-start.1 = (f32[36,36,2,128]{3,1,2,0:T(8,128)}, f32[36,36,2,128]{3,1,2,0:T(8,128)}, u32[]{:S(2)}, u32[]{:S(2)}) collective-permute-start(f32[36,36,2,128]{3,1,2,0:T(8,128)} %copy.111), channel_id=1, source_target_pairs={{4,0},{8,4},{12,8},{16,12},{20,16},{24,20},{28,24},{32,28},{36,32}... | collective-permute-start | bytes 3981320 | tf_op jit(solution)/shard_map/ppermute | solution.py:25
  13.0 34.4 %collective-permute-start = (f32[36,36,2,128]{3,1,2,0:T(8,128)}, f32[36,36,2,128]{3,1,2,0:T(8,128)}, u32[]{:S(2)}, u32[]{:S(2)}) collective-permute-start(f32[36,36,2,128]{3,1,2,0:T(8,128)} %copy.110), channel_id=1, source_target_pairs={{0,4},{4,8},{8,12},{12,16},{16,20},{20,24},{24,28},{28,32},{32,36}... | collective-permute-start | bytes 3981320 | tf_op jit(solution)/shard_map/ppermute | solution.py:24
  15.4 20.4 %all-to-all-start = ((f32[2,32,6]{2,0,1:T(2,128)}), f32[2,32,6]{2,0,1:T(2,128)S(1)}, u32[]{:S(2)}, u32[]{:S(2)}) async-start(f32[2,32,6]{2,0,1:T(2,128)} %copy.105), calls=%async_computation | async-start | bytes 65536 | tf_op jit(solution)/shard_map/all_to_all | solution.py:75
  86.5 3.8 %copy-start = (f32[36,36,4,128]{1,0,3,2:T(8,128)}, f32[36,36,4,128]{1,0,3,2:T(8,128)S(1)}, u32[]{:S(2)}) copy-start(f32[36,36,4,128]{1,0,3,2:T(8,128)S(1)} %fusion.20) | copy-start | bytes 7962628
  90.4 7.1 %collective-permute-start.2 = (f32[36,36,4,2]{1,0,3,2:T(8,128)S(1)}, f32[36,36,4,2]{1,0,3,2:T(8,128)S(1)}, u32[]{:S(2)}, u32[]{:S(2)}) collective-permute-start(f32[36,36,4,2]{1,0,3,2:T(8,128)S(1)} %get-tuple-element.16), channel_id=1, source_target_pairs={{0,1},{1,2},{2,3},{4,5},{5,6},{6,7},{8,9},{9,10},{10,11},{12,13},{... | collective-permute-start | bytes 124424 | tf_op jit(solution)/shard_map/ppermute | solution.py:24
  93.8 7.8 %collective-permute-start.3 = (f32[36,36,4,2]{1,0,3,2:T(8,128)S(1)}, f32[36,36,4,2]{1,0,3,2:T(8,128)S(1)}, u32[]{:S(2)}, u32[]{:S(2)}) collective-permute-start(f32[36,36,4,2]{1,0,3,2:T(8,128)S(1)} %get-tuple-element.17), channel_id=1, source_target_pairs={{1,0},{2,1},{3,2},{5,4},{6,5},{7,6},{9,8},{10,9},{11,10},{13,12},{... | collective-permute-start | bytes 124424 | tf_op jit(solution)/shard_map/ppermute | solution.py:25
where the time goes:
time: 200 us; the launch traced here: 199 us
  other arithmetic  108 us (54%)
  local copies, waits for them, and re-layouts  61.7 us (31%)
  starting transfers between devices  17.4 us (9%)
  waiting for transfers between devices  10.5 us (5%)
    mul x2, other arithmetic, transport(): courant * (upwind + 0.5 * (1.0 - magnitude) * (downwind - upwind) - (1.0...  44.3 us
    unnamed x21, local copies, waits for them, and re-layouts  22.2 us
    reduce_sum x1, other arithmetic, local(): energy = jnp.mean(refracted, axis=(0, 1))  18.3 us
    mul x1, other arithmetic, local(): spectrum_next = refracted * jnp.exp(growth - decay_rate)  11.1 us
    add x1, other arithmetic, local(): jnp.maximum(face_speed, 0.0) * density  10.9 us
    mul x1, other arithmetic, local(): density = (density - transport(padded, courant_lat, 3)) * sea_frac  10.9 us
    mul x1, other arithmetic, local(): density = (density - transport(padded, courant_lon, 2)) * sea_frac  10.8 us
    slice x1, local copies, waits for them, and re-layouts, local(): refracted = density - (face_flux - jnp.roll(face_flux, 1, axis=1))  10.6 us
  transfers between devices with their start and end apart: 5, of which 3 were waited for; matrix products, arithmetic and copies ran while one was open for 12% of the time, Pallas kernels for 0%

commit v1 on v0

v1 whole, which is shorter than its diff:
```python
import functools
import math

import jax
import jax.numpy as jnp
import numpy as np
from jax import lax
from jax.experimental import pallas as pl
from jax.experimental.pallas import tpu as pltpu
from jax.sharding import PartitionSpec as P

FREQ = 36
DIRS = 36
QUAD = 9
LANES = 128
CELLS = 4
CAP = 6
BLOCKS = ((0, 8), (8, 8), (16, 8), (24, 8), (32, 4))
LOG2E = math.log2(math.e)
MESH = pl.DeviceIdType.MESH


def tables():
    k = np.arange(FREQ, dtype=np.float64)
    freq = 0.035 * 1.1**k
    ratio = 0.035 / freq
    rel = freq / freq[-1]
    slow = 2.0 * math.pi * freq / 9.81
    rows = np.stack(
        [0.9 * ratio, np.sqrt(ratio), LOG2E * 0.05 * rel * slow, LOG2E * 0.05 * rel]
    )
    per_freq = np.broadcast_to(rows[:, :, None], (4, FREQ, LANES)).astype(np.float32)
    decay = (LOG2E * 0.8 * rel * 4.0).astype(np.float32)
    theta = (np.arange(DIRS) + 0.5) * 2.0 * math.pi / DIRS
    phi = (np.arange(DIRS) + 1.0) * 2.0 * math.pi / DIRS
    per_dir = np.stack([np.cos(theta), np.sin(theta), np.sin(phi), np.cos(phi)], axis=1)
    return per_freq, per_dir.astype(np.float32), decay


def coefficients(rate, speed):
    a = rate * speed
    third = a * a * (1.0 / 6.0)
    g = a * (third - 1.0 / 6.0)
    b = a * ((third + 1.0 / 3.0) - 0.5 * a)
    p1 = (a - b) - (g + g)
    p0 = (1.0 - p1) - (g - b)
    return p0, p1, g, b


def take(table, index):
    return jnp.take_along_axis(table, index, axis=1, mode="promise_in_bounds")


def exchange_kernel(
    lon_size,
    lat_size,
    spec,
    sea_hbm,
    refr_hbm,
    atm_hbm,
    hour_hbm,
    cells_hbm,
    slots_hbm,
    weights_hbm,
    freq_hbm,
    dirs,
    out,
    energy_out,
    wind_out,
    xb,
    halo,
    packed,
    lat_in,
    merged,
    g_prev,
    e_sum,
    sea_i,
    refr,
    atm,
    hour,
    cells,
    slots,
    weights,
    freq,
    sea_b,
    r0_b,
    r1_b,
    u_b,
    v_b,
    wsend,
    wrecv,
    in_sem,
    x_sem,
    lon_send,
    lon_recv,
    lat_send,
    lat_recv,
    w_send,
    w_recv,
):
    me = lax.axis_index("lon")
    la = lax.axis_index("lat")
    right = lax.rem(me + 1, lon_size)
    left = lax.rem(me + lon_size - 1, lon_size)
    north = lax.rem(la + 1, lat_size)
    south = lax.rem(la + lat_size - 1, lat_size)

    barrier = pltpu.get_barrier_semaphore()

    def greet(d, carry):
        pl.semaphore_signal(
            barrier, inc=1, device_id=(lax.rem(me + d, lon_size), la), device_id_type=MESH
        )
        return carry

    lax.fori_loop(1, lon_size, greet, 0)
    for peer in (north, south):
        pl.semaphore_signal(barrier, inc=1, device_id=(me, peer), device_id_type=MESH)

    small = [
        (atm_hbm, atm),
        (hour_hbm, hour),
        (cells_hbm, cells),
        (sea_hbm, sea_i),
        (refr_hbm, refr),
        (slots_hbm, slots),
        (weights_hbm, weights),
        (freq_hbm, freq),
    ]
    small = [
        pltpu.make_async_copy(src, dst, in_sem.at[i]) for i, (src, dst) in enumerate(small)
    ]
    for copy in small:
        copy.start()

    def load(j, carry):
        for x in range(CELLS):
            pltpu.make_async_copy(spec.at[:, j, x, 0, :], xb.at[j, x], x_sem.at[j, x]).start()
        return carry

    lax.fori_loop(0, DIRS, load, 0)
    pl.semaphore_wait(barrier, lon_size + 1)

    def send_lon(j, x, slot, peer):
        pltpu.make_async_remote_copy(
            src_ref=spec.at[:, j, x, 0, :],
            dst_ref=halo.at[j, slot],
            send_sem=lon_send.at[j, slot],
            recv_sem=lon_recv.at[j, slot],
            device_id=(peer, la),
            device_id_type=MESH,
        ).start()

    def send_forward(j, carry):
        send_lon(j, 3, 0, right)
        send_lon(j, 0, 1, left)
        send_lon(j, 2, 2, right)
        return carry

    def send_backward(j, carry):
        send_lon(j, 3, 0, right)
        send_lon(j, 0, 1, left)
        send_lon(j, 1, 2, left)
        return carry

    lax.fori_loop(0, QUAD, send_forward, 0)
    lax.fori_loop(QUAD, 3 * QUAD, send_backward, 0)
    lax.fori_loop(3 * QUAD, DIRS, send_forward, 0)

    for copy in small:
        copy.wait()

    late = hour[0]
    wind = (1.0 - late) * atm[0] + late * atm[1]
    row = lax.broadcasted_iota(jnp.int32, (32, LANES), 0)
    lane32 = lax.broadcasted_iota(jnp.int32, (32, LANES), 1)
    six = lane32 - (lane32 // CAP) * CAP
    place = row * CAP + six
    tail = jnp.concatenate([cells[:, LANES:], jnp.zeros((1, 64), jnp.int32)], axis=1)
    head_b = jnp.broadcast_to(cells[:, :LANES], (32, LANES))
    tail_b = jnp.broadcast_to(tail, (32, LANES))
    low = take(head_b, jnp.minimum(place, LANES - 1))
    high = take(tail_b, jnp.maximum(place - LANES, 0))
    index = jnp.where(place < LANES, low, high)
    u_pick = take(jnp.broadcast_to(wind[0:1], (32, LANES)), index)
    v_pick = take(jnp.broadcast_to(wind[1:2], (32, LANES)), index)
    pick = jnp.where(lane32 < CAP, u_pick, v_pick)
    for i in range(32):
        wsend[i] = pick[i : i + 1]

    def send_wind(d, carry):
        peer = lax.rem(me + d, lon_size)
        pltpu.make_async_remote_copy(
            src_ref=wsend.at[peer],
            dst_ref=wrecv.at[me],
            send_sem=w_send.at[peer],
            recv_sem=w_recv.at[me],
            device_id=(peer, la),
            device_id_type=MESH,
        ).start()
        return carry

    lax.fori_loop(1, lon_size, send_wind, 0)
    wrecv[me] = wsend[me]

    sea = sea_i[...].astype(jnp.float32)
    r0 = refr[0]
    r1 = refr[1]
    for x in range(CELLS):
        sea_b[x] = jnp.broadcast_to(sea[x : x + 1], (8, LANES))
        r0_b[x] = jnp.broadcast_to(r0[x : x + 1], (8, LANES))
        r1_b[x] = jnp.broadcast_to(r1[x : x + 1], (8, LANES))
    e_sum[...] = jnp.zeros_like(e_sum)

    lane = lax.broadcasted_iota(jnp.int32, (8, LANES), 1)
    lane_three = lane - (lane // 3) * 3
    first = lane == 0
    last = lane == LANES - 1

    def lon_step(q):
        lon_forward = q in (0, 3)
        lat_forward = q < 2
        shift = 2 if lat_forward else 1
        packed[q] = jnp.zeros((FREQ, LANES), jnp.float32)

        def body(jl, carry):
            j = q * QUAD + jl
            for x in range(CELLS):
                pltpu.make_async_copy(spec.at[:, j, x, 0, :], xb.at[j, x], x_sem.at[j, x]).wait()
            for slot in range(3):
                pltpu.make_async_copy(
                    halo.at[j, slot], halo.at[j, slot], lon_recv.at[j, slot]
                ).wait()
            speed = dirs[j, 0] if lon_forward else -dirs[j, 0]
            base = jl * (3 * CELLS)
            for k0, n in BLOCKS:
                ks = pl.ds(k0, n)
                p0, p1, p2, pd = coefficients(freq[0, ks], speed)
                before = halo[j, 0, ks]
                after = halo[j, 1, ks]
                far = halo[j, 2, ks]
                own = [xb[j, x, ks] for x in range(CELLS)]
                if lon_forward:
                    line = [far, before] + own + [after]
                else:
                    line = [far, after] + own[::-1] + [before]
                pack = packed[q, ks]
                for i in range(CELLS):
                    x = i if lon_forward else CELLS - 1 - i
                    value = (p0 * line[i + 2] + p1 * line[i + 1]) + (
                        p2 * line[i] - pd * line[i + 3]
                    )
                    value = value * sea_b[x, :n]
                    xb[j, x, ks] = value
                    start = base + 3 * x
                    offset = lane[:n] - start
                    inside = (offset >= 0) & (offset < 3)
                    pack = jnp.where(inside, pltpu.roll(value, start + shift, 1), pack)
                packed[q, ks] = pack
            return carry

        lax.fori_loop(0, QUAD, body, 0)
        for side, peer in enumerate((north, south)):
            pltpu.make_async_remote_copy(
                src_ref=packed.at[q],
                dst_ref=lat_in.at[q, side],
                send_sem=lat_send.at[q, side],
                recv_sem=lat_recv.at[q, side],
                device_id=(me, peer),
                device_id_type=MESH,
            ).start()

    has_south = (la > 0).astype(jnp.float32)
    has_north = (la < lat_size - 1).astype(jnp.float32)

    def refract(jp, x, k0, n, here, ahead, behind):
        ks = pl.ds(k0, n)
        rate = r0_b[x, :n] * dirs[jp, 2] - r1_b[x, :n] * dirs[jp, 3]
        flux = (freq[1, ks] * rate) * jnp.where(rate > 0.0, here, ahead)
        return flux, (here - flux) + behind

    def growth(jp, x, k0, n):
        ks = pl.ds(k0, n)
        along = u_b[x, :n] * dirs[jp, 0] + v_b[x, :n] * dirs[jp, 1]
        return jnp.exp2(jnp.maximum(freq[2, ks] * along - freq[3, ks], 0.0))

    def put(j, x, k0, n, value):
        out[pl.ds(k0 * (DIRS * CELLS) + j * CELLS + x, n, stride=DIRS * CELLS), :] = value

    def lat_step(q):
        lat_forward = q < 2
        for side, peer in enumerate((north, south)):
            pltpu.make_async_copy(
                lat_in.at[q, side], lat_in.at[q, side], lat_recv.at[q, side]
            ).wait()
        for k0, n in BLOCKS:
            ks = pl.ds(k0, n)
            from_south = lat_in[q, 0, ks] * has_south
            from_north = lat_in[q, 1, ks] * has_north
            if lat_forward:
                value = jnp.where(lane_three[:n] == 2, from_north, from_south)
            else:
                value = jnp.where(lane_three[:n] == 0, from_south, from_north)
            merged[ks] = value

        def body(jl, carry):
            j = q * QUAD + jl
            jp = jnp.maximum(j - 1, 0)
            speed = dirs[j, 1] if lat_forward else -dirs[j, 1]
            base = jl * (3 * CELLS)
            for k0, n in BLOCKS:
                ks = pl.ds(k0, n)
                p0, p1, p2, pd = coefficients(freq[0, ks], speed)
                window = merged[ks]
                for x in range(CELLS):
                    start = base + 3 * x
                    f = xb[j, x, ks]
                    if lat_forward:
                        w = pltpu.roll(window, LANES + 126 - start, 1)
                        up2 = pltpu.roll(jnp.where(lane[:n] >= 126, w, f), 2, 1)
                        up1 = pltpu.roll(jnp.where(last[:n], w, f), 1, 1)
                        down = pltpu.roll(jnp.where(first[:n], w, f), 127, 1)
                    else:
                        w = pltpu.roll(window, LANES + 127 - start, 1)
                        up2 = pltpu.roll(jnp.where(lane[:n] < 2, w, f), 126, 1)
                        up1 = pltpu.roll(jnp.where(first[:n], w, f), 127, 1)
                        down = pltpu.roll(jnp.where(last[:n], w, f), 1, 1)
                    value = (p0 * f + p1 * up1) + (p2 * up2 - pd * down)
                    value = value * sea_b[x, :n]
                    xb[j, x, ks] = value
                    e_sum[x, ks] += value
                    flux, moved = refract(jp, x, k0, n, xb[jp, x, ks], value, g_prev[x, ks])
                    g_prev[x, ks] = flux
                    put(jp, x, k0, n, moved * growth(jp, x, k0, n))
            return carry

        lax.fori_loop(0, QUAD, body, 0)

    def finish_wind():
        def arrive(d, carry):
            peer = lax.rem(me + d, lon_size)
            pltpu.make_async_copy(wrecv.at[peer], wrecv.at[peer], w_recv.at[peer]).wait()
            return carry

        lax.fori_loop(1, lon_size, arrive, 0)
        table = jnp.concatenate([wrecv[i] for i in range(32)], axis=0)
        halves = []
        for part in range(2):
            spot = lane32 + part * LANES
            source = spot // CAP
            q = spot - source * CAP
            mine = source == row
            for comp in range(2):
                got = jnp.where(mine, take(table, q + comp * CAP), 0.0)
                halves.append(jnp.sum(got, axis=0, keepdims=True))
        slot = slots[...]
        low_slot = jnp.minimum(slot, LANES - 1)
        high_slot = jnp.maximum(slot - LANES, 0)
        winds = []
        for comp in range(2):
            low_b = jnp.broadcast_to(halves[comp], (16, LANES))
            high_b = jnp.broadcast_to(halves[2 + comp], (16, LANES))
            got = jnp.where(slot < LANES, take(low_b, low_slot), take(high_b, high_slot))
            got = got * weights[...]
            half = got[0:8] + got[8:16]
            winds.append(half[0:4] + half[4:8])
        wind_out[0] = winds[0]
        wind_out[1] = winds[1]
        for x in range(CELLS):
            u_b[x] = jnp.broadcast_to(winds[0][x : x + 1], (8, LANES))
            v_b[x] = jnp.broadcast_to(winds[1][x : x + 1], (8, LANES))

    lon_step(0)
    lon_step(1)
    finish_wind()
    lat_step(0)
    lon_step(2)
    lat_step(1)
    lon_step(3)
    lat_step(2)
    lat_step(3)

    for k0, n in BLOCKS:
        ks = pl.ds(k0, n)
        for x in range(CELLS):
            f0 = xb[0, x, ks]
            f_last = xb[DIRS - 1, x, ks]
            flux, moved = refract(DIRS - 1, x, k0, n, f_last, f0, g_prev[x, ks])
            put(DIRS - 1, x, k0, n, moved * growth(DIRS - 1, x, k0, n))
            _, moved = refract(0, x, k0, n, f0, xb[1, x, ks], flux)
            put(0, x, k0, n, moved * growth(0, x, k0, n))
    for x in range(CELLS):
        energy = jnp.sum(e_sum[x], axis=0, keepdims=True) * (1.0 / (FREQ * DIRS))
        energy_out[x : x + 1] = energy
        energy_out[x + 4 : x + 5] = energy

    def sent(j, carry):
        for slot in range(3):
            pltpu.make_async_copy(
                spec.at[:, j, 0, 0, :], halo.at[j, slot], lon_send.at[j, slot]
            ).wait()
        return carry

    lax.fori_loop(0, DIRS, sent, 0)
    for q in range(4):
        for side in range(2):
            pltpu.make_async_copy(packed.at[q], packed.at[q], lat_send.at[q, side]).wait()
    def wind_sent(d, carry):
        peer = lax.rem(me + d, lon_size)
        pltpu.make_async_copy(wsend.at[peer], wsend.at[peer], w_send.at[peer]).wait()
        return carry

    lax.fori_loop(1, lon_size, wind_sent, 0)


CHUNK = 4


def finish_kernel(moved, energy, wind, decay, out, wind_out, stage, wstage, sem, wsem):
    wstage[...] = wind[...]
    wcopy = pltpu.make_async_copy(wstage, wind_out, wsem)
    wcopy.start()
    e = energy[...]
    square = e * e

    def copy(c):
        ks = pl.ds(c * CHUNK, CHUNK)
        return pltpu.make_async_copy(stage.at[ks], out.at[ks], sem.at[c])

    def chunk(c, carry):
        for i in range(CHUNK):
            k = c * CHUNK + i
            factor = jnp.exp2(-(decay[k] * square))
            stage[k] = moved[k] * factor[None]
        copy(c).start()
        return carry

    lax.fori_loop(0, FREQ // CHUNK, chunk, 0)
    for c in range(FREQ // CHUNK):
        copy(c).wait()
    wcopy.wait()


def local(
    lon_size,
    lat_size,
    spectrum,
    sea_mask,
    refraction,
    atm_wind,
    hour_fraction,
    send_cells,
    recv_slots,
    recv_weights,
):
    per_freq, per_dir, decay = tables()
    f32 = jnp.float32
    hbm = pl.BlockSpec(memory_space=pltpu.HBM)
    vmem = pl.BlockSpec(memory_space=pltpu.VMEM)
    smem = pl.BlockSpec(memory_space=pltpu.SMEM)
    moved, energy, wind = pl.pallas_call(
        functools.partial(exchange_kernel, lon_size, lat_size),
        name="exchange",
        out_shape=(
            pltpu.VMEM((FREQ * DIRS * CELLS, LANES), f32),
            pltpu.VMEM((8, LANES), f32),
            pltpu.VMEM((2, CELLS, LANES), f32),
        ),
        in_specs=[hbm] * 9 + [smem],
        out_specs=(vmem, vmem, vmem),
        scratch_shapes=[
            pltpu.VMEM((DIRS, CELLS, FREQ, LANES), f32),
            pltpu.VMEM((DIRS, 3, FREQ, LANES), f32),
            pltpu.VMEM((4, FREQ, LANES), f32),
            pltpu.VMEM((4, 2, FREQ, LANES), f32),
            pltpu.VMEM((FREQ, LANES), f32),
            pltpu.VMEM((CELLS, FREQ, LANES), f32),
            pltpu.VMEM((CELLS, FREQ, LANES), f32),
            pltpu.VMEM((CELLS, LANES), jnp.int32),
            pltpu.VMEM((2, CELLS, LANES), f32),
            pltpu.VMEM((2, 2, LANES), f32),
            pltpu.SMEM((1,), f32),
            pltpu.VMEM((1, 192), jnp.int32),
            pltpu.VMEM((16, LANES), jnp.int32),
            pltpu.VMEM((16, LANES), f32),
            pltpu.VMEM((4, FREQ, LANES), f32),
            pltpu.VMEM((CELLS, 8, LANES), f32),
            pltpu.VMEM((CELLS, 8, LANES), f32),
            pltpu.VMEM((CELLS, 8, LANES), f32),
            pltpu.VMEM((CELLS, 8, LANES), f32),
            pltpu.VMEM((CELLS, 8, LANES), f32),
            pltpu.VMEM((32, 1, LANES), f32),
            pltpu.VMEM((32, 1, LANES), f32),
            pltpu.SemaphoreType.DMA((8,)),
            pltpu.SemaphoreType.DMA((DIRS, CELLS)),
            pltpu.SemaphoreType.DMA((DIRS, 3)),
            pltpu.SemaphoreType.DMA((DIRS, 3)),
            pltpu.SemaphoreType.DMA((4, 2)),
            pltpu.SemaphoreType.DMA((4, 2)),
            pltpu.SemaphoreType.DMA((32,)),
            pltpu.SemaphoreType.DMA((32,)),
        ],
        compiler_params=pltpu.CompilerParams(
            collective_id=0, has_side_effects=True, vmem_limit_bytes=54 << 20
        ),
    )(
        spectrum.reshape(FREQ, DIRS, CELLS, 1, LANES),
        sea_mask,
        refraction,
        atm_wind,
        hour_fraction,
        send_cells,
        recv_slots.reshape(4 * CELLS, LANES),
        recv_weights.reshape(4 * CELLS, LANES),
        jnp.asarray(per_freq),
        jnp.asarray(per_dir),
    )
    result, wind = pl.pallas_call(
        finish_kernel,
        name="finish",
        out_shape=(
            jax.ShapeDtypeStruct((FREQ, DIRS // 2, 8, LANES), f32),
            jax.ShapeDtypeStruct((2, CELLS, LANES), f32),
        ),
        in_specs=[vmem, vmem, vmem, smem],
        out_specs=(hbm, hbm),
        scratch_shapes=[
            pltpu.VMEM((FREQ, DIRS // 2, 8, LANES), f32),
            pltpu.VMEM((2, CELLS, LANES), f32),
            pltpu.SemaphoreType.DMA((FREQ // CHUNK,)),
            pltpu.SemaphoreType.DMA,
        ],
        compiler_params=pltpu.CompilerParams(vmem_limit_bytes=40 << 20),
    )(moved.reshape(FREQ, DIRS // 2, 8, LANES), energy, wind, jnp.asarray(decay))
    return result.reshape(FREQ, DIRS, CELLS, LANES), wind


def solution(mesh):
    in_specs = (
        P(None, None, "lon", "lat"),
        P("lon", "lat"),
        P(None, "lon", "lat"),
        P(None, None, ("lon", "lat")),
        P(),
        P(("lon", "lat"), None),
        P(None, "lon", "lat"),
        P(None, "lon", "lat"),
    )
    out_specs = (P(None, None, "lon", "lat"), P(None, "lon", "lat"))
    body = functools.partial(local, mesh.shape["lon"], mesh.shape["lat"])
    return jax.shard_map(body, mesh=mesh, in_specs=in_specs, out_specs=out_specs, check_vma=False)
```

time: 200 us -> 45.2 us (0.23)
  other arithmetic: 108 us -> 0 us
  local copies, waits for them, and re-layouts: 61.7 us -> 0.01 us
  Pallas kernels: 0 us -> 43.5 us
  starting transfers between devices: 17.4 us -> 0 us
  waiting for transfers between devices: 10.5 us -> 0 us
    mul x11 -> x0, other arithmetic: 78 us -> none  [the longest x2 44.3 us: transport(): courant * (upwind + 0.5 * (1.0 - magnitude) * (downwind - upwind) - (1.0...]
    pallas_call x0 -> x2, Pallas kernels: none -> 43.5 us  [the longest x1 41.4 us: local(): pl.pallas_call(functools.partial(exchange_kernel, lon_size, lat_size), na...]
    unnamed x21 -> x2, local copies, waits for them, and re-layouts: 22.2 us -> 0.01 us
    slice x6 -> x0, local copies, waits for them, and re-layouts: 21.9 us -> none  [the longest x1 10.6 us: local(): refracted = density - (face_flux - jnp.roll(face_flux, 1, axis=1))]
    reduce_sum x2 -> x0, other arithmetic: 18.6 us -> none  [the longest x1 18.3 us: local(): energy = jnp.mean(refracted, axis=(0, 1))]
    add x3 -> x0, other arithmetic: 11.1 us -> none  [the longest x1 10.9 us: local(): jnp.maximum(face_speed, 0.0) * density]
    ppermute x4 -> x0, starting transfers between devices: 10.7 us -> none  [the longest x2 7.3 us: padded_2(): after = lax.ppermute(initial, axis, down)]
    ppermute x2 -> x0, local copies, waits for them, and re-layouts: 10.3 us -> none  [the longest x1 5.22 us: padded_2(): after = lax.ppermute(initial, axis, down)]
  transfers between devices with their start and end apart: 5 -> 0, of which waited for: 3 -> 0; matrix products, arithmetic and copies ran while one was open for 12% -> 0% of each run, Pallas kernels for 0% -> 0%
where the time goes in v1:
time: 45.2 us; the launch traced here: 44.9 us
  Pallas kernels  43.5 us (96%)
  between operations  1.31 us (3%)
    pallas_call x1, Pallas kernels, local(): pl.pallas_call(functools.partial(exchange_kernel, lon_size, lat_size), na...  41.4 us
    pallas_call x1, Pallas kernels, local(): pl.pallas_call(finish_kernel, name='finish', out_shape=(jax.ShapeDtypeStr...  2.15 us

profile of v1, /device:TPU:0, one launch (start us, length us, event | category | flops | bytes accessed | tf_op | source)
XLA Modules:
  0.0 44.9 jit_solution(2140699786049042765)
XLA Ops:
  0.6 0.0 copy-start
  1.3 41.4 %exchange.1 = (f32[5184,128]{1,0:T(8,128)S(1)}, f32[8,128]{1,0:T(8,128)S(1)}, f32[2,4,128]{2,1,0:T(4,128)S(1)}) custom-call(f32[36,36,4,1,128]{4,3,2,1,0:T(1,128)} %bitcast.6, s32[4,128]{1,0:T(4,128)} %sea_hbm.1, f32[2,4,128]{2,1,0:T(4,128)} %refr_hbm.1, f32[2,2,128]{2,1,0:T(2,128)} %atm_hbm.1, f32[1]{0:T(128)S(6)} %copy.13.hour_hbm, s32[1,192]{1,0:T(1,128)} %cells_hbm.1, ...), custom_call_target="tpu_custom_call" | custom-call | tf_op jit(solution)/shard_map/exchange/pallas_call | solution.py:461
  42.7 0.0 copy-done
  42.7 2.2 %finish.1 = (f32[36,18,8,128]{3,2,1,0:T(8,128)}, f32[2,4,128]{2,1,0:T(4,128)}) custom-call(f32[36,18,8,128]{3,2,1,0:T(8,128)S(1)} %bitcast.5, f32[8,128]{1,0:T(8,128)S(1)} %get-tuple-element.8.energy, f32[2,4,128]{2,1,0:T(4,128)S(1)} %get-tuple-element.9.wind, f32[36]{0:T(128)S(1)} %copy-done), custom_call_target="tpu_custom_call" | custom-call | tf_op jit(solution)/shard_map/finish/pallas_call | solution.py:518
Async XLA Ops:
  0.6 42.1 %copy-start = (f32[36]{0:T(128)S(1)}, f32[36]{0:T(128)}, u32[]{:S(2)}) copy-start(f32[36]{0:T(128)} %constant.8.clone.decay) | copy-start | bytes 436

commit v2 on v1

--- a/solution.py
+++ b/solution.py
@@ -12,6 +12,9 @@
 FREQ = 36
 DIRS = 36
 QUAD = 9
+SPAN = 3
+GROUPS = 3
+EDGE = 12
 LANES = 128
 CELLS = 4
 CAP = 6
@@ -34,7 +37,7 @@
     theta = (np.arange(DIRS) + 0.5) * 2.0 * math.pi / DIRS
     phi = (np.arange(DIRS) + 1.0) * 2.0 * math.pi / DIRS
     per_dir = np.stack([np.cos(theta), np.sin(theta), np.sin(phi), np.cos(phi)], axis=1)
-    return per_freq, per_dir.astype(np.float32), decay
+    return per_freq, per_dir.reshape(-1).astype(np.float32), decay
 
 
 def coefficients(rate, speed):
@@ -55,10 +58,11 @@
     lon_size,
     lat_size,
     spec,
+    spec_rows,
     sea_hbm,
     refr_hbm,
     atm_hbm,
-    hour_hbm,
+    hour,
     cells_hbm,
     slots_hbm,
     weights_hbm,
@@ -67,6 +71,7 @@
     out,
     energy_out,
     wind_out,
+    nat,
     xb,
     halo,
     packed,
@@ -77,7 +82,6 @@
     sea_i,
     refr,
     atm,
-    hour,
     cells,
     slots,
     weights,
@@ -119,7 +123,6 @@
 
     small = [
         (atm_hbm, atm),
-        (hour_hbm, hour),
         (cells_hbm, cells),
         (sea_hbm, sea_i),
         (refr_hbm, refr),
@@ -133,20 +136,16 @@
     for copy in small:
         copy.start()
 
-    def load(j, carry):
-        for x in range(CELLS):
-            pltpu.make_async_copy(spec.at[:, j, x, 0, :], xb.at[j, x], x_sem.at[j, x]).start()
-        return carry
-
-    lax.fori_loop(0, DIRS, load, 0)
+    whole = pltpu.make_async_copy(spec_rows, nat, x_sem)
+    whole.start()
     pl.semaphore_wait(barrier, lon_size + 1)
 
     def send_lon(j, x, slot, peer):
         pltpu.make_async_remote_copy(
             src_ref=spec.at[:, j, x, 0, :],
-            dst_ref=halo.at[j, slot],
-            send_sem=lon_send.at[j, slot],
-            recv_sem=lon_recv.at[j, slot],
+            dst_ref=halo.at[j // SPAN, (j % SPAN) * 3 + slot],
+            send_sem=lon_send,
+            recv_sem=lon_recv.at[j // SPAN],
             device_id=(peer, la),
             device_id_type=MESH,
         ).start()
@@ -164,8 +163,6 @@
         return carry
 
     lax.fori_loop(0, QUAD, send_forward, 0)
-    lax.fori_loop(QUAD, 3 * QUAD, send_backward, 0)
-    lax.fori_loop(3 * QUAD, DIRS, send_forward, 0)
 
     for copy in small:
         copy.wait()
@@ -193,14 +190,16 @@
         pltpu.make_async_remote_copy(
             src_ref=wsend.at[peer],
             dst_ref=wrecv.at[me],
-            send_sem=w_send.at[peer],
-            recv_sem=w_recv.at[me],
+            send_sem=w_send,
+            recv_sem=w_recv,
             device_id=(peer, la),
             device_id_type=MESH,
         ).start()
         return carry
 
     lax.fori_loop(1, lon_size, send_wind, 0)
+    lax.fori_loop(QUAD, 3 * QUAD, send_backward, 0)
+    lax.fori_loop(3 * QUAD, DIRS, send_forward, 0)
     wrecv[me] = wsend[me]
 
     sea = sea_i[...].astype(jnp.float32)
@@ -217,34 +216,30 @@
     first = lane == 0
     last = lane == LANES - 1
 
-    def lon_step(q):
+    def rows_of(j, x, k0, n):
+        return pl.ds(k0 * (DIRS * CELLS) + j * CELLS + x, n, stride=DIRS * CELLS)
+
+    def lon_group(q, g):
         lon_forward = q in (0, 3)
-        lat_forward = q < 2
-        shift = 2 if lat_forward else 1
-        packed[q] = jnp.zeros((FREQ, LANES), jnp.float32)
+        shift = 2 if q < 2 else 1
+        group = q * GROUPS + g
+        pltpu.make_async_copy(halo.at[group], halo.at[group], lon_recv.at[group]).wait()
 
         def body(jl, carry):
-            j = q * QUAD + jl
-            for x in range(CELLS):
-                pltpu.make_async_copy(spec.at[:, j, x, 0, :], xb.at[j, x], x_sem.at[j, x]).wait()
-            for slot in range(3):
-                pltpu.make_async_copy(
-                    halo.at[j, slot], halo.at[j, slot], lon_recv.at[j, slot]
-                ).wait()
-            speed = dirs[j, 0] if lon_forward else -dirs[j, 0]
-            base = jl * (3 * CELLS)
+            j = group * SPAN + jl
+            speed = dirs[4 * j] if lon_forward else -dirs[4 * j]
             for k0, n in BLOCKS:
                 ks = pl.ds(k0, n)
                 p0, p1, p2, pd = coefficients(freq[0, ks], speed)
-                before = halo[j, 0, ks]
-                after = halo[j, 1, ks]
-                far = halo[j, 2, ks]
-                own = [xb[j, x, ks] for x in range(CELLS)]
+                before = halo[group, 3 * jl, ks]
+                after = halo[group, 3 * jl + 1, ks]
+                far = halo[group, 3 * jl + 2, ks]
+                own = [nat[rows_of(j, x, k0, n), :] for x in range(CELLS)]
                 if lon_forward:
                     line = [far, before] + own + [after]
                 else:
                     line = [far, after] + own[::-1] + [before]
-                pack = packed[q, ks]
+                pack = pltpu.roll(packed[group, ks], EDGE, 1)
                 for i in range(CELLS):
                     x = i if lon_forward else CELLS - 1 - i
                     value = (p0 * line[i + 2] + p1 * line[i + 1]) + (
@@ -252,20 +247,18 @@
                     )
                     value = value * sea_b[x, :n]
                     xb[j, x, ks] = value
-                    start = base + 3 * x
-                    offset = lane[:n] - start
-                    inside = (offset >= 0) & (offset < 3)
-                    pack = jnp.where(inside, pltpu.roll(value, start + shift, 1), pack)
-                packed[q, ks] = pack
+                    inside = (lane[:n] >= 3 * x) & (lane[:n] < 3 * x + 3)
+                    pack = jnp.where(inside, pltpu.roll(value, 3 * x + shift, 1), pack)
+                packed[group, ks] = pack
             return carry
 
-        lax.fori_loop(0, QUAD, body, 0)
+        lax.fori_loop(0, SPAN, body, 0)
         for side, peer in enumerate((north, south)):
             pltpu.make_async_remote_copy(
-                src_ref=packed.at[q],
-                dst_ref=lat_in.at[q, side],
-                send_sem=lat_send.at[q, side],
-                recv_sem=lat_recv.at[q, side],
+                src_ref=packed.at[group],
+                dst_ref=lat_in.at[group, side],
+                send_sem=lat_send.at[side],
+                recv_sem=lat_recv.at[group],
                 device_id=(me, peer),
                 device_id_type=MESH,
             ).start()
@@ -273,55 +266,58 @@
     has_south = (la > 0).astype(jnp.float32)
     has_north = (la < lat_size - 1).astype(jnp.float32)
 
-    def refract(jp, x, k0, n, here, ahead, behind):
+    def rows_at(jp):
+        d = [dirs[4 * jp + i] for i in range(4)]
+        rates = [r0_b[x] * d[2] - r1_b[x] * d[3] for x in range(CELLS)]
+        signs = [rate > 0.0 for rate in rates]
+        along = [u_b[x] * d[0] + v_b[x] * d[1] for x in range(CELLS)]
+        return rates, signs, along
+
+    def refract(rows, x, k0, n, here, ahead, behind):
+        rates, signs, _ = rows
+        flux = (freq[1, pl.ds(k0, n)] * rates[x][:n]) * jnp.where(signs[x][:n], here, ahead)
+        return flux, (here - flux) + behind
+
+    def growth(rows, x, k0, n):
         ks = pl.ds(k0, n)
-        rate = r0_b[x, :n] * dirs[jp, 2] - r1_b[x, :n] * dirs[jp, 3]
-        flux = (freq[1, ks] * rate) * jnp.where(rate > 0.0, here, ahead)
-        return flux, (here - flux) + behind
-
-    def growth(jp, x, k0, n):
-        ks = pl.ds(k0, n)
-        along = u_b[x, :n] * dirs[jp, 0] + v_b[x, :n] * dirs[jp, 1]
-        return jnp.exp2(jnp.maximum(freq[2, ks] * along - freq[3, ks], 0.0))
+        return jnp.exp2(jnp.maximum(freq[2, ks] * rows[2][x][:n] - freq[3, ks], 0.0))
 
     def put(j, x, k0, n, value):
-        out[pl.ds(k0 * (DIRS * CELLS) + j * CELLS + x, n, stride=DIRS * CELLS), :] = value
-
-    def lat_step(q):
+        out[rows_of(j, x, k0, n), :] = value
+
+    def lat_group(q, g):
         lat_forward = q < 2
-        for side, peer in enumerate((north, south)):
-            pltpu.make_async_copy(
-                lat_in.at[q, side], lat_in.at[q, side], lat_recv.at[q, side]
-            ).wait()
+        group = q * GROUPS + g
+        pltpu.make_async_copy(lat_in.at[group], lat_in.at[group], lat_recv.at[group]).wait()
         for k0, n in BLOCKS:
             ks = pl.ds(k0, n)
-            from_south = lat_in[q, 0, ks] * has_south
-            from_north = lat_in[q, 1, ks] * has_north
+            from_south = lat_in[group, 0, ks] * has_south
+            from_north = lat_in[group, 1, ks] * has_north
             if lat_forward:
                 value = jnp.where(lane_three[:n] == 2, from_north, from_south)
             else:
                 value = jnp.where(lane_three[:n] == 0, from_south, from_north)
-            merged[ks] = value
+            merged[ks] = pltpu.roll(value, LANES - EDGE * (SPAN - 1), 1)
 
         def body(jl, carry):
-            j = q * QUAD + jl
+            j = group * SPAN + jl
             jp = jnp.maximum(j - 1, 0)
-            speed = dirs[j, 1] if lat_forward else -dirs[j, 1]
-            base = jl * (3 * CELLS)
+            speed = dirs[4 * j + 1] if lat_forward else -dirs[4 * j + 1]
+            rows = rows_at(jp)
             for k0, n in BLOCKS:
                 ks = pl.ds(k0, n)
                 p0, p1, p2, pd = coefficients(freq[0, ks], speed)
                 window = merged[ks]
+                merged[ks] = pltpu.roll(window, EDGE, 1)
                 for x in range(CELLS):
-                    start = base + 3 * x
                     f = xb[j, x, ks]
                     if lat_forward:
-                        w = pltpu.roll(window, LANES + 126 - start, 1)
+                        w = pltpu.roll(window, 126 - 3 * x, 1)
                         up2 = pltpu.roll(jnp.where(lane[:n] >= 126, w, f), 2, 1)
                         up1 = pltpu.roll(jnp.where(last[:n], w, f), 1, 1)
                         down = pltpu.roll(jnp.where(first[:n], w, f), 127, 1)
                     else:
-                        w = pltpu.roll(window, LANES + 127 - start, 1)
+                        w = pltpu.roll(window, 127 - 3 * x, 1)
                         up2 = pltpu.roll(jnp.where(lane[:n] < 2, w, f), 126, 1)
                         up1 = pltpu.roll(jnp.where(first[:n], w, f), 127, 1)
                         down = pltpu.roll(jnp.where(last[:n], w, f), 1, 1)
@@ -329,20 +325,15 @@
                     value = value * sea_b[x, :n]
                     xb[j, x, ks] = value
                     e_sum[x, ks] += value
-                    flux, moved = refract(jp, x, k0, n, xb[jp, x, ks], value, g_prev[x, ks])
+                    flux, moved = refract(rows, x, k0, n, xb[jp, x, ks], value, g_prev[x, ks])
                     g_prev[x, ks] = flux
-                    put(jp, x, k0, n, moved * growth(jp, x, k0, n))
+                    put(jp, x, k0, n, moved * growth(rows, x, k0, n))
             return carry
 
-        lax.fori_loop(0, QUAD, body, 0)
+        lax.fori_loop(0, SPAN, body, 0)
 
     def finish_wind():
-        def arrive(d, carry):
-            peer = lax.rem(me + d, lon_size)
-            pltpu.make_async_copy(wrecv.at[peer], wrecv.at[peer], w_recv.at[peer]).wait()
-            return carry
-
-        lax.fori_loop(1, lon_size, arrive, 0)
+        pltpu.make_async_copy(wrecv.at[pl.ds(0, 31)], wrecv.at[pl.ds(0, 31)], w_recv).wait()
         table = jnp.concatenate([wrecv[i] for i in range(32)], axis=0)
         halves = []
         for part in range(2):
@@ -370,47 +361,42 @@
             u_b[x] = jnp.broadcast_to(winds[0][x : x + 1], (8, LANES))
             v_b[x] = jnp.broadcast_to(winds[1][x : x + 1], (8, LANES))
 
-    lon_step(0)
-    lon_step(1)
+    def stage(q):
+        def body(g, carry):
+            if q < 4:
+                lon_group(q, g)
+            if q > 0:
+                lat_group(q - 1, g)
+            return carry
+
+        lax.fori_loop(0, GROUPS, body, 0)
+
+    whole.wait()
+    stage(0)
     finish_wind()
-    lat_step(0)
-    lon_step(2)
-    lat_step(1)
-    lon_step(3)
-    lat_step(2)
-    lat_step(3)
-
+    for q in range(1, 5):
+        stage(q)
+
+    rows_last = rows_at(DIRS - 1)
+    rows_first = rows_at(0)
     for k0, n in BLOCKS:
         ks = pl.ds(k0, n)
         for x in range(CELLS):
             f0 = xb[0, x, ks]
             f_last = xb[DIRS - 1, x, ks]
-            flux, moved = refract(DIRS - 1, x, k0, n, f_last, f0, g_prev[x, ks])
-            put(DIRS - 1, x, k0, n, moved * growth(DIRS - 1, x, k0, n))
-            _, moved = refract(0, x, k0, n, f0, xb[1, x, ks], flux)
-            put(0, x, k0, n, moved * growth(0, x, k0, n))
+            flux, moved = refract(rows_last, x, k0, n, f_last, f0, g_prev[x, ks])
+            put(DIRS - 1, x, k0, n, moved * growth(rows_last, x, k0, n))
+            _, moved = refract(rows_first, x, k0, n, f0, xb[1, x, ks], flux)
+            put(0, x, k0, n, moved * growth(rows_first, x, k0, n))
     for x in range(CELLS):
         energy = jnp.sum(e_sum[x], axis=0, keepdims=True) * (1.0 / (FREQ * DIRS))
         energy_out[x : x + 1] = energy
         energy_out[x + 4 : x + 5] = energy
 
-    def sent(j, carry):
-        for slot in range(3):
-            pltpu.make_async_copy(
-                spec.at[:, j, 0, 0, :], halo.at[j, slot], lon_send.at[j, slot]
-            ).wait()
-        return carry
-
-    lax.fori_loop(0, DIRS, sent, 0)
-    for q in range(4):
-        for side in range(2):
-            pltpu.make_async_copy(packed.at[q], packed.at[q], lat_send.at[q, side]).wait()
-    def wind_sent(d, carry):
-        peer = lax.rem(me + d, lon_size)
-        pltpu.make_async_copy(wsend.at[peer], wsend.at[peer], w_send.at[peer]).wait()
-        return carry
-
-    lax.fori_loop(1, lon_size, wind_sent, 0)
+    pltpu.make_async_copy(halo, halo, lon_send).wait()
+    for side in range(2):
+        pltpu.make_async_copy(packed, packed, lat_send.at[side]).wait()
+    pltpu.make_async_copy(wsend.at[pl.ds(0, 31)], wsend.at[pl.ds(0, 31)], w_send).wait()
 
 
 CHUNK = 4
@@ -466,20 +452,20 @@
             pltpu.VMEM((8, LANES), f32),
             pltpu.VMEM((2, CELLS, LANES), f32),
         ),
-        in_specs=[hbm] * 9 + [smem],
+        in_specs=[hbm] * 5 + [smem] + [hbm] * 4 + [smem],
         out_specs=(vmem, vmem, vmem),
         scratch_shapes=[
+            pltpu.VMEM((FREQ * DIRS * CELLS, LANES), f32),
             pltpu.VMEM((DIRS, CELLS, FREQ, LANES), f32),
-            pltpu.VMEM((DIRS, 3, FREQ, LANES), f32),
-            pltpu.VMEM((4, FREQ, LANES), f32),
-            pltpu.VMEM((4, 2, FREQ, LANES), f32),
+            pltpu.VMEM((4 * GROUPS, 3 * SPAN, FREQ, LANES), f32),
+            pltpu.VMEM((4 * GROUPS, FREQ, LANES), f32),
+            pltpu.VMEM((4 * GROUPS, 2, FREQ, LANES), f32),
             pltpu.VMEM((FREQ, LANES), f32),
             pltpu.VMEM((CELLS, FREQ, LANES), f32),
             pltpu.VMEM((CELLS, FREQ, LANES), f32),
             pltpu.VMEM((CELLS, LANES), jnp.int32),
             pltpu.VMEM((2, CELLS, LANES), f32),
             pltpu.VMEM((2, 2, LANES), f32),
-            pltpu.SMEM((1,), f32),
             pltpu.VMEM((1, 192), jnp.int32),
             pltpu.VMEM((16, LANES), jnp.int32),
             pltpu.VMEM((16, LANES), f32),
@@ -491,20 +477,21 @@
             pltpu.VMEM((CELLS, 8, LANES), f32),
             pltpu.VMEM((32, 1, LANES), f32),
             pltpu.VMEM((32, 1, LANES), f32),
-            pltpu.SemaphoreType.DMA((8,)),
-            pltpu.SemaphoreType.DMA((DIRS, CELLS)),
-            pltpu.SemaphoreType.DMA((DIRS, 3)),
-            pltpu.SemaphoreType.DMA((DIRS, 3)),
-            pltpu.SemaphoreType.DMA((4, 2)),
-            pltpu.SemaphoreType.DMA((4, 2)),
-            pltpu.SemaphoreType.DMA((32,)),
-            pltpu.SemaphoreType.DMA((32,)),
+            pltpu.SemaphoreType.DMA((7,)),
+            pltpu.SemaphoreType.DMA,
+            pltpu.SemaphoreType.DMA,
+            pltpu.SemaphoreType.DMA((4 * GROUPS,)),
+            pltpu.SemaphoreType.DMA((2,)),
+            pltpu.SemaphoreType.DMA((4 * GROUPS,)),
+            pltpu.SemaphoreType.DMA,
+            pltpu.SemaphoreType.DMA,
         ],
         compiler_params=pltpu.CompilerParams(
             collective_id=0, has_side_effects=True, vmem_limit_bytes=54 << 20
         ),
     )(
         spectrum.reshape(FREQ, DIRS, CELLS, 1, LANES),
+        spectrum.reshape(FREQ * DIRS * CELLS, LANES),
         sea_mask,
         refraction,
         atm_wind,

time: 45.2 us -> 35.2 us (0.78)
  Pallas kernels: 43.5 us -> 33.8 us
    pallas_call x1, Pallas kernels: 41.4 us -> 31.7 us  [local(): pl.pallas_call(functools.partial(exchange_kernel, lon_size, lat_size), na...]
where the time goes in v2:
time: 35.2 us; the launch traced here: 35.1 us
  Pallas kernels  33.8 us (96%)
  between operations  1.3 us (4%)
    pallas_call x1, Pallas kernels, local(): pl.pallas_call(functools.partial(exchange_kernel, lon_size, lat_size), na...  31.7 us
    pallas_call x1, Pallas kernels, local(): pl.pallas_call(finish_kernel, name='finish', out_shape=(jax.ShapeDtypeStr...  2.15 us

profile of v2, /device:TPU:0, one launch (start us, length us, event | category | flops | bytes accessed | tf_op | source)
XLA Modules:
  0.0 35.1 jit_solution(11706579759249152531)
XLA Ops:
  1.3 0.0 copy-start
  1.3 31.7 %exchange.1 = (f32[5184,128]{1,0:T(8,128)S(1)}, f32[8,128]{1,0:T(8,128)S(1)}, f32[2,4,128]{2,1,0:T(4,128)S(1)}) custom-call(f32[36,36,4,1,128]{4,3,2,1,0:T(1,128)} %bitcast.7, f32[5184,128]{1,0:T(8,128)} %bitcast.8, s32[4,128]{1,0:T(4,128)} %sea_hbm.1, f32[2,4,128]{2,1,0:T(4,128)} %refr_hbm.1, f32[2,2,128]{2,1,0:T(2,128)} %atm_hbm.1, f32[1]{0:T(128)S(6)} %copy.13.hour, ...), custom_call_target="tpu_custom_call" | custom-call | tf_op jit(solution)/shard_map/exchange/pallas_call | solution.py:447
  33.0 0.0 copy-done
  33.0 2.2 %finish.1 = (f32[36,18,8,128]{3,2,1,0:T(8,128)}, f32[2,4,128]{2,1,0:T(4,128)}) custom-call(f32[36,18,8,128]{3,2,1,0:T(8,128)S(1)} %bitcast.6, f32[8,128]{1,0:T(8,128)S(1)} %get-tuple-element.8.energy, f32[2,4,128]{2,1,0:T(4,128)S(1)} %get-tuple-element.9.wind, f32[36]{0:T(128)S(1)} %copy-done), custom_call_target="tpu_custom_call" | custom-call | tf_op jit(solution)/shard_map/finish/pallas_call | solution.py:505
Async XLA Ops:
  1.3 31.7 %copy-start = (f32[36]{0:T(128)S(1)}, f32[36]{0:T(128)}, u32[]{:S(2)}) copy-start(f32[36]{0:T(128)} %constant.8.clone.decay) | copy-start | bytes 436

commit v3 on v2

--- a/solution.py
+++ b/solution.py
@@ -14,7 +14,8 @@
 QUAD = 9
 SPAN = 3
 GROUPS = 3
-EDGE = 12
+SIDE = 4
+EDGE = SIDE * 4
 LANES = 128
 CELLS = 4
 CAP = 6
@@ -72,7 +73,9 @@
     energy_out,
     wind_out,
     nat,
-    xb,
+    along_lon,
+    field,
+    f_prev,
     halo,
     packed,
     lat_in,
@@ -212,47 +215,53 @@
     e_sum[...] = jnp.zeros_like(e_sum)
 
     lane = lax.broadcasted_iota(jnp.int32, (8, LANES), 1)
-    lane_three = lane - (lane // 3) * 3
-    first = lane == 0
-    last = lane == LANES - 1
+    spot_all = lane & (SIDE - 1)
+    edge = (lane >= LANES - 2) | (lane < 2)
 
     def rows_of(j, x, k0, n):
         return pl.ds(k0 * (DIRS * CELLS) + j * CELLS + x, n, stride=DIRS * CELLS)
 
-    def lon_group(q, g):
-        lon_forward = q in (0, 3)
-        shift = 2 if q < 2 else 1
-        group = q * GROUPS + g
+    def lon_wait(group):
         pltpu.make_async_copy(halo.at[group], halo.at[group], lon_recv.at[group]).wait()
 
+    def lon_cells(lon_forward, group, jl):
+        j = group * SPAN + jl
+        speed = dirs[4 * j] if lon_forward else -dirs[4 * j]
+        for k0, n in BLOCKS:
+            ks = pl.ds(k0, n)
+            p0, p1, p2, pd = coefficients(freq[0, ks], speed)
+            before = halo[group, 3 * jl, ks]
+            after = halo[group, 3 * jl + 1, ks]
+            far = halo[group, 3 * jl + 2, ks]
+            own = [nat[rows_of(j, x, k0, n), :] for x in range(CELLS)]
+            if lon_forward:
+                line = [far, before] + own + [after]
+            else:
+                line = [far, after] + own[::-1] + [before]
+            pack = pltpu.roll(packed[group, ks], EDGE, 1)
+            for i in range(CELLS):
+                x = i if lon_forward else CELLS - 1 - i
+                value = (p0 * line[i + 2] + p1 * line[i + 1]) + (
+                    p2 * line[i] - pd * line[i + 3]
+                )
+                value = value * sea_b[x, :n]
+                along_lon[j, x, ks] = value
+                start = SIDE * x
+                inside = (lane[:n] >= start) & (lane[:n] < start + SIDE)
+                pack = jnp.where(inside, pltpu.roll(value, start + 2, 1), pack)
+            packed[group, ks] = pack
+
+    def lon_group(lon_forward, group):
+        lon_wait(group)
+
         def body(jl, carry):
-            j = group * SPAN + jl
-            speed = dirs[4 * j] if lon_forward else -dirs[4 * j]
-            for k0, n in BLOCKS:
-                ks = pl.ds(k0, n)
-                p0, p1, p2, pd = coefficients(freq[0, ks], speed)
-                before = halo[group, 3 * jl, ks]
-                after = halo[group, 3 * jl + 1, ks]
-                far = halo[group, 3 * jl + 2, ks]
-                own = [nat[rows_of(j, x, k0, n), :] for x in range(CELLS)]
-                if lon_forward:
-                    line = [far, before] + own + [after]
-                else:
-                    line = [far, after] + own[::-1] + [before]
-                pack = pltpu.roll(packed[group, ks], EDGE, 1)
-                for i in range(CELLS):
-                    x = i if lon_forward else CELLS - 1 - i
-                    value = (p0 * line[i + 2] + p1 * line[i + 1]) + (
-                        p2 * line[i] - pd * line[i + 3]
-                    )
-                    value = value * sea_b[x, :n]
-                    xb[j, x, ks] = value
-                    inside = (lane[:n] >= 3 * x) & (lane[:n] < 3 * x + 3)
-                    pack = jnp.where(inside, pltpu.roll(value, 3 * x + shift, 1), pack)
-                packed[group, ks] = pack
+            lon_cells(lon_forward, group, jl)
             return carry
 
         lax.fori_loop(0, SPAN, body, 0)
+        lat_send_edges(group)
+
+    def lat_send_edges(group):
         for side, peer in enumerate((north, south)):
             pltpu.make_async_remote_copy(
                 src_ref=packed.at[group],
@@ -285,49 +294,59 @@
     def put(j, x, k0, n, value):
         out[rows_of(j, x, k0, n), :] = value
 
-    def lat_group(q, g):
-        lat_forward = q < 2
-        group = q * GROUPS + g
+    def lat_prepare(lat_forward, group):
         pltpu.make_async_copy(lat_in.at[group], lat_in.at[group], lat_recv.at[group]).wait()
+        j = group * SPAN
+        sign = 1.0 if lat_forward else -1.0
+        speeds = [sign * dirs[4 * (j + i) + 1] for i in range(SPAN)]
+        speed = jnp.where(lane < EDGE, speeds[2], jnp.where(lane < 2 * EDGE, speeds[1], speeds[0]))
         for k0, n in BLOCKS:
             ks = pl.ds(k0, n)
+            spot = spot_all[:n]
             from_south = lat_in[group, 0, ks] * has_south
             from_north = lat_in[group, 1, ks] * has_north
-            if lat_forward:
-                value = jnp.where(lane_three[:n] == 2, from_north, from_south)
-            else:
-                value = jnp.where(lane_three[:n] == 0, from_south, from_north)
+            _, p1, p2, pd = coefficients(freq[0, ks], speed[:n])
+            value = jnp.where(spot < 2, from_south, from_north) - packed[group, ks]
+            one = 1 if lat_forward else LANES - 1
+            near, next_spot, down_spot = (2, 3, 1) if lat_forward else (1, 0, 2)
+            up_one = pltpu.roll(value, one, 1)
+            up_two = pltpu.roll(value, (2 * one) % LANES, 1)
+            down = pltpu.roll(value, LANES - one, 1)
+            value = p2 * jnp.where((spot == near) | (spot == next_spot), up_two, 0.0)
+            value = value + p1 * jnp.where(spot == near, up_one, 0.0)
+            value = value - pd * jnp.where(spot == down_spot, down, 0.0)
             merged[ks] = pltpu.roll(value, LANES - EDGE * (SPAN - 1), 1)
 
+    def lat_cells(lat_forward, group, jl):
+        j = group * SPAN + jl
+        jp = jnp.maximum(j - 1, 0)
+        speed = dirs[4 * j + 1] if lat_forward else -dirs[4 * j + 1]
+        rows = rows_at(jp)
+        two, one = (2, LANES - 1) if lat_forward else (LANES - 2, 1)
+        for k0, n in BLOCKS:
+            ks = pl.ds(k0, n)
+            p0, p1, p2, pd = coefficients(freq[0, ks], speed)
+            window = merged[ks]
+            merged[ks] = pltpu.roll(window, EDGE, 1)
+            for x in range(CELLS):
+                f = along_lon[j, x, ks]
+                extra = jnp.where(edge[:n], pltpu.roll(window, LANES - 2 - SIDE * x, 1), 0.0)
+                shifted = pltpu.roll(f, two, 1)
+                odd = pltpu.roll(p1 * shifted - pd * f, one, 1)
+                value = (odd + extra) + (p0 * f + p2 * shifted)
+                value = value * sea_b[x, :n]
+                field[j, x, ks] = value
+                e_sum[x, ks] += value
+                flux, moved = refract(rows, x, k0, n, f_prev[x, ks], value, g_prev[x, ks])
+                f_prev[x, ks] = value
+                g_prev[x, ks] = flux
+                put(jp, x, k0, n, moved * growth(rows, x, k0, n))
+
+    def lat_group(lat_forward, group):
+        lat_prepare(lat_forward, group)
+
         def body(jl, carry):
-            j = group * SPAN + jl
-            jp = jnp.maximum(j - 1, 0)
-            speed = dirs[4 * j + 1] if lat_forward else -dirs[4 * j + 1]
-            rows = rows_at(jp)
-            for k0, n in BLOCKS:
-                ks = pl.ds(k0, n)
-                p0, p1, p2, pd = coefficients(freq[0, ks], speed)
-                window = merged[ks]
-                merged[ks] = pltpu.roll(window, EDGE, 1)
-                for x in range(CELLS):
-                    f = xb[j, x, ks]
-                    if lat_forward:
-                        w = pltpu.roll(window, 126 - 3 * x, 1)
-                        up2 = pltpu.roll(jnp.where(lane[:n] >= 126, w, f), 2, 1)
-                        up1 = pltpu.roll(jnp.where(last[:n], w, f), 1, 1)
-                        down = pltpu.roll(jnp.where(first[:n], w, f), 127, 1)
-                    else:
-                        w = pltpu.roll(window, 127 - 3 * x, 1)
-                        up2 = pltpu.roll(jnp.where(lane[:n] < 2, w, f), 126, 1)
-                        up1 = pltpu.roll(jnp.where(first[:n], w, f), 127, 1)
-                        down = pltpu.roll(jnp.where(last[:n], w, f), 1, 1)
-                    value = (p0 * f + p1 * up1) + (p2 * up2 - pd * down)
-                    value = value * sea_b[x, :n]
-                    xb[j, x, ks] = value
-                    e_sum[x, ks] += value
-                    flux, moved = refract(rows, x, k0, n, xb[jp, x, ks], value, g_prev[x, ks])
-                    g_prev[x, ks] = flux
-                    put(jp, x, k0, n, moved * growth(rows, x, k0, n))
+            lat_cells(lat_forward, group, jl)
             return carry
 
         lax.fori_loop(0, SPAN, body, 0)
@@ -361,37 +380,62 @@
             u_b[x] = jnp.broadcast_to(winds[0][x : x + 1], (8, LANES))
             v_b[x] = jnp.broadcast_to(winds[1][x : x + 1], (8, LANES))
 
-    def stage(q):
-        def body(g, carry):
-            if q < 4:
-                lon_group(q, g)
-            if q > 0:
-                lat_group(q - 1, g)
-            return carry
-
-        lax.fori_loop(0, GROUPS, body, 0)
-
     whole.wait()
-    stage(0)
-    finish_wind()
-    for q in range(1, 5):
-        stage(q)
-
-    rows_last = rows_at(DIRS - 1)
-    rows_first = rows_at(0)
-    for k0, n in BLOCKS:
-        ks = pl.ds(k0, n)
-        for x in range(CELLS):
-            f0 = xb[0, x, ks]
-            f_last = xb[DIRS - 1, x, ks]
-            flux, moved = refract(rows_last, x, k0, n, f_last, f0, g_prev[x, ks])
-            put(DIRS - 1, x, k0, n, moved * growth(rows_last, x, k0, n))
-            _, moved = refract(rows_first, x, k0, n, f0, xb[1, x, ks], flux)
-            put(0, x, k0, n, moved * growth(rows_first, x, k0, n))
-    for x in range(CELLS):
+
+    def run(g, carry):
+        turn = (g >= GROUPS) & (g < 3 * GROUPS)
+
+        @pl.when((g < 4 * GROUPS) & jnp.logical_not(turn))
+        def _():
+            lon_group(True, g)
+
+        @pl.when(turn)
+        def _():
+            lon_group(False, g)
+
+        @pl.when(g == GROUPS)
+        def _():
+            finish_wind()
+
+        @pl.when(turn)
+        def _():
+            lat_group(True, g - GROUPS)
+
+        @pl.when(g >= 3 * GROUPS)
+        def _():
+            lat_group(False, g - GROUPS)
+
+        return carry
+
+    lax.fori_loop(0, 5 * GROUPS, run, 0)
+
+    def close(x, carry):
+        def row_of(jp):
+            d = [dirs[4 * jp + i] for i in range(4)]
+            return r0_b[x] * d[2] - r1_b[x] * d[3], u_b[x] * d[0] + v_b[x] * d[1]
+
+        rate_last, along_last = row_of(DIRS - 1)
+        rate_first, along_first = row_of(0)
+        for k0, n in BLOCKS:
+            ks = pl.ds(k0, n)
+            f0 = field[0, x, ks]
+            f_last = f_prev[x, ks]
+            f1 = field[1, x, ks]
+            bend = freq[1, ks]
+            flux = (bend * rate_last[:n]) * jnp.where(rate_last[:n] > 0.0, f_last, f0)
+            moved = (f_last - flux) + g_prev[x, ks]
+            grow = jnp.exp2(jnp.maximum(freq[2, ks] * along_last[:n] - freq[3, ks], 0.0))
+            put(DIRS - 1, x, k0, n, moved * grow)
+            flux0 = (bend * rate_first[:n]) * jnp.where(rate_first[:n] > 0.0, f0, f1)
+            moved = (f0 - flux0) + flux
+            grow = jnp.exp2(jnp.maximum(freq[2, ks] * along_first[:n] - freq[3, ks], 0.0))
+            put(0, x, k0, n, moved * grow)
         energy = jnp.sum(e_sum[x], axis=0, keepdims=True) * (1.0 / (FREQ * DIRS))
-        energy_out[x : x + 1] = energy
-        energy_out[x + 4 : x + 5] = energy
+        energy_out[pl.ds(x, 1)] = energy
+        energy_out[pl.ds(x + 4, 1)] = energy
+        return carry
+
+    lax.fori_loop(0, CELLS, close, 0)
 
     pltpu.make_async_copy(halo, halo, lon_send).wait()
     for side in range(2):
@@ -457,6 +501,8 @@
         scratch_shapes=[
             pltpu.VMEM((FREQ * DIRS * CELLS, LANES), f32),
             pltpu.VMEM((DIRS, CELLS, FREQ, LANES), f32),
+            pltpu.VMEM((DIRS, CELLS, FREQ, LANES), f32),
+            pltpu.VMEM((CELLS, FREQ, LANES), f32),
             pltpu.VMEM((4 * GROUPS, 3 * SPAN, FREQ, LANES), f32),
             pltpu.VMEM((4 * GROUPS, FREQ, LANES), f32),
             pltpu.VMEM((4 * GROUPS, 2, FREQ, LANES), f32),

time: 35.2 us -> 33.5 us (0.952)
  Pallas kernels: 33.8 us -> 32 us
    pallas_call x1, Pallas kernels: 31.7 us -> 29.9 us  [local(): pl.pallas_call(functools.partial(exchange_kernel, lon_size, lat_size), na...]
where the time goes in v3:
time: 33.5 us; the launch traced here: 33.3 us
  Pallas kernels  32 us (96%)
  between operations  1.3 us (4%)
    pallas_call x1, Pallas kernels, local(): pl.pallas_call(functools.partial(exchange_kernel, lon_size, lat_size), na...  29.9 us
    pallas_call x1, Pallas kernels, local(): pl.pallas_call(finish_kernel, name='finish', out_shape=(jax.ShapeDtypeStr...  2.15 us

profile of v3, /device:TPU:0, one launch (start us, length us, event | category | flops | bytes accessed | tf_op | source)
XLA Modules:
  0.0 33.3 jit_solution(1001324667808132177)
XLA Ops:
  1.3 0.0 copy-start
  1.3 29.9 %exchange.1 = (f32[5184,128]{1,0:T(8,128)S(1)}, f32[8,128]{1,0:T(8,128)S(1)}, f32[2,4,128]{2,1,0:T(4,128)S(1)}) custom-call(f32[36,36,4,1,128]{4,3,2,1,0:T(1,128)} %bitcast.7, f32[5184,128]{1,0:T(8,128)} %bitcast.8, s32[4,128]{1,0:T(4,128)} %sea_hbm.1, f32[2,4,128]{2,1,0:T(4,128)} %refr_hbm.1, f32[2,2,128]{2,1,0:T(2,128)} %atm_hbm.1, f32[1]{0:T(128)S(6)} %copy.13.hour, ...), custom_call_target="tpu_custom_call" | custom-call | tf_op jit(solution)/shard_map/exchange/pallas_call | solution.py:491
  31.2 0.0 copy-done
  31.2 2.2 %finish.1 = (f32[36,18,8,128]{3,2,1,0:T(8,128)}, f32[2,4,128]{2,1,0:T(4,128)}) custom-call(f32[36,18,8,128]{3,2,1,0:T(8,128)S(1)} %bitcast.6, f32[8,128]{1,0:T(8,128)S(1)} %get-tuple-element.8.energy, f32[2,4,128]{2,1,0:T(4,128)S(1)} %get-tuple-element.9.wind, f32[36]{0:T(128)S(1)} %copy-done), custom_call_target="tpu_custom_call" | custom-call | tf_op jit(solution)/shard_map/finish/pallas_call | solution.py:551
Async XLA Ops:
  1.3 29.9 %copy-start = (f32[36]{0:T(128)S(1)}, f32[36]{0:T(128)}, u32[]{:S(2)}) copy-start(f32[36]{0:T(128)} %constant.8.clone.decay) | copy-start | bytes 436

commit v4 on v3

--- a/solution.py
+++ b/solution.py
@@ -20,6 +20,10 @@
 CELLS = 4
 CAP = 6
 BLOCKS = ((0, 8), (8, 8), (16, 8), (24, 8), (32, 4))
+FIRST = 2
+DEPTH = 12
+CLOSING = (DIRS - 2, DIRS - 1, 0)
+LAG = 5
 LOG2E = math.log2(math.e)
 MESH = pl.DeviceIdType.MESH
 
@@ -76,6 +80,7 @@
     along_lon,
     field,
     f_prev,
+    coef,
     halo,
     packed,
     lat_in,
@@ -153,19 +158,22 @@
             device_id_type=MESH,
         ).start()
 
-    def send_forward(j, carry):
-        send_lon(j, 3, 0, right)
-        send_lon(j, 0, 1, left)
-        send_lon(j, 2, 2, right)
+    def send_group(group, carry):
+        turned = (group >= GROUPS) & (group < 3 * GROUPS)
+        cell = jnp.where(turned, 1, 2)
+        peer = jnp.where(turned, left, right)
+
+        def one(jl, inner):
+            j = group * SPAN + jl
+            send_lon(j, 3, 0, right)
+            send_lon(j, 0, 1, left)
+            send_lon(j, cell, 2, peer)
+            return inner
+
+        lax.fori_loop(0, SPAN, one, 0)
         return carry
 
-    def send_backward(j, carry):
-        send_lon(j, 3, 0, right)
-        send_lon(j, 0, 1, left)
-        send_lon(j, 1, 2, left)
-        return carry
-
-    lax.fori_loop(0, QUAD, send_forward, 0)
+    lax.fori_loop(0, FIRST, send_group, 0)
 
     for copy in small:
         copy.wait()
@@ -201,8 +209,6 @@
         return carry
 
     lax.fori_loop(1, lon_size, send_wind, 0)
-    lax.fori_loop(QUAD, 3 * QUAD, send_backward, 0)
-    lax.fori_loop(3 * QUAD, DIRS, send_forward, 0)
     wrecv[me] = wsend[me]
 
     sea = sea_i[...].astype(jnp.float32)
@@ -226,10 +232,9 @@
 
     def lon_cells(lon_forward, group, jl):
         j = group * SPAN + jl
-        speed = dirs[4 * j] if lon_forward else -dirs[4 * j]
         for k0, n in BLOCKS:
             ks = pl.ds(k0, n)
-            p0, p1, p2, pd = coefficients(freq[0, ks], speed)
+            p0, p1, p2, pd = (coef[j, i, ks] for i in range(4))
             before = halo[group, 3 * jl, ks]
             after = halo[group, 3 * jl + 1, ks]
             far = halo[group, 3 * jl + 2, ks]
@@ -319,13 +324,12 @@
 
     def lat_cells(lat_forward, group, jl):
         j = group * SPAN + jl
-        jp = jnp.maximum(j - 1, 0)
-        speed = dirs[4 * j + 1] if lat_forward else -dirs[4 * j + 1]
+        jp = jnp.maximum(j - 2, 0)
         rows = rows_at(jp)
         two, one = (2, LANES - 1) if lat_forward else (LANES - 2, 1)
         for k0, n in BLOCKS:
             ks = pl.ds(k0, n)
-            p0, p1, p2, pd = coefficients(freq[0, ks], speed)
+            p0, p1, p2, pd = (coef[j, 4 + i, ks] for i in range(4))
             window = merged[ks]
             merged[ks] = pltpu.roll(window, EDGE, 1)
             for x in range(CELLS):
@@ -335,18 +339,25 @@
                 odd = pltpu.roll(p1 * shifted - pd * f, one, 1)
                 value = (odd + extra) + (p0 * f + p2 * shifted)
                 value = value * sea_b[x, :n]
-                field[j, x, ks] = value
+                here, ahead = f_prev[1, x, ks], f_prev[0, x, ks]
+                flux, moved = refract(rows, x, k0, n, here, ahead, g_prev[x, ks])
+                put(jp, x, k0, n, moved * growth(rows, x, k0, n))
+                g_prev[x, ks] = flux
+                f_prev[1, x, ks] = ahead
+                f_prev[0, x, ks] = value
                 e_sum[x, ks] += value
-                flux, moved = refract(rows, x, k0, n, f_prev[x, ks], value, g_prev[x, ks])
-                f_prev[x, ks] = value
-                g_prev[x, ks] = flux
-                put(jp, x, k0, n, moved * growth(rows, x, k0, n))
 
     def lat_group(lat_forward, group):
         lat_prepare(lat_forward, group)
 
         def body(jl, carry):
             lat_cells(lat_forward, group, jl)
+            if lat_forward:
+
+                @pl.when(group * SPAN + jl < 2)
+                def _():
+                    field[group * SPAN + jl] = f_prev[0]
+
             return carry
 
         lax.fori_loop(0, SPAN, body, 0)
@@ -380,10 +391,26 @@
             u_b[x] = jnp.broadcast_to(winds[0][x : x + 1], (8, LANES))
             v_b[x] = jnp.broadcast_to(winds[1][x : x + 1], (8, LANES))
 
+    lax.fori_loop(FIRST, DEPTH, send_group, 0)
+
+    def prepare(j, carry):
+        for k0, n in BLOCKS:
+            ks = pl.ds(k0, n)
+            for axis in range(2):
+                speed = jnp.abs(jnp.full((n, LANES), dirs[4 * j + axis], jnp.float32))
+                for i, value in enumerate(coefficients(freq[0, ks], speed)):
+                    coef[j, 4 * axis + i, ks] = value
+        return carry
+
+    lax.fori_loop(0, DIRS, prepare, 0)
     whole.wait()
 
     def run(g, carry):
         turn = (g >= GROUPS) & (g < 3 * GROUPS)
+
+        @pl.when(g < 4 * GROUPS - DEPTH)
+        def _():
+            send_group(g + DEPTH, 0)
 
         @pl.when((g < 4 * GROUPS) & jnp.logical_not(turn))
         def _():
@@ -393,43 +420,40 @@
         def _():
             lon_group(False, g)
 
-        @pl.when(g == GROUPS)
+        @pl.when(g == LAG)
         def _():
             finish_wind()
 
-        @pl.when(turn)
+        @pl.when((g >= LAG) & (g < LAG + 2 * GROUPS))
         def _():
-            lat_group(True, g - GROUPS)
-
-        @pl.when(g >= 3 * GROUPS)
+            lat_group(True, g - LAG)
+
+        @pl.when(g >= LAG + 2 * GROUPS)
         def _():
-            lat_group(False, g - GROUPS)
+            lat_group(False, g - LAG)
 
         return carry
 
-    lax.fori_loop(0, 5 * GROUPS, run, 0)
+    lax.fori_loop(0, 4 * GROUPS + LAG, run, 0)
 
     def close(x, carry):
         def row_of(jp):
             d = [dirs[4 * jp + i] for i in range(4)]
             return r0_b[x] * d[2] - r1_b[x] * d[3], u_b[x] * d[0] + v_b[x] * d[1]
 
-        rate_last, along_last = row_of(DIRS - 1)
-        rate_first, along_first = row_of(0)
+        rows = [row_of(jp) for jp in CLOSING]
         for k0, n in BLOCKS:
             ks = pl.ds(k0, n)
             f0 = field[0, x, ks]
-            f_last = f_prev[x, ks]
-            f1 = field[1, x, ks]
-            bend = freq[1, ks]
-            flux = (bend * rate_last[:n]) * jnp.where(rate_last[:n] > 0.0, f_last, f0)
-            moved = (f_last - flux) + g_prev[x, ks]
-            grow = jnp.exp2(jnp.maximum(freq[2, ks] * along_last[:n] - freq[3, ks], 0.0))
-            put(DIRS - 1, x, k0, n, moved * grow)
-            flux0 = (bend * rate_first[:n]) * jnp.where(rate_first[:n] > 0.0, f0, f1)
-            moved = (f0 - flux0) + flux
-            grow = jnp.exp2(jnp.maximum(freq[2, ks] * along_first[:n] - freq[3, ks], 0.0))
-            put(0, x, k0, n, moved * grow)
+            line = (f_prev[1, x, ks], f_prev[0, x, ks], f0, field[1, x, ks])
+            flux = g_prev[x, ks]
+            for i, jp in enumerate(CLOSING):
+                rate, along = (part[:n] for part in rows[i])
+                now = (freq[1, ks] * rate) * jnp.where(rate > 0.0, line[i], line[i + 1])
+                moved = (line[i] - now) + flux
+                grow = jnp.exp2(jnp.maximum(freq[2, ks] * along - freq[3, ks], 0.0))
+                put(jp, x, k0, n, moved * grow)
+                flux = now
         energy = jnp.sum(e_sum[x], axis=0, keepdims=True) * (1.0 / (FREQ * DIRS))
         energy_out[pl.ds(x, 1)] = energy
         energy_out[pl.ds(x + 4, 1)] = energy
@@ -501,8 +525,9 @@
         scratch_shapes=[
             pltpu.VMEM((FREQ * DIRS * CELLS, LANES), f32),
             pltpu.VMEM((DIRS, CELLS, FREQ, LANES), f32),
-            pltpu.VMEM((DIRS, CELLS, FREQ, LANES), f32),
-            pltpu.VMEM((CELLS, FREQ, LANES), f32),
+            pltpu.VMEM((2, CELLS, FREQ, LANES), f32),
+            pltpu.VMEM((2, CELLS, FREQ, LANES), f32),
+            pltpu.VMEM((DIRS, 8, FREQ, LANES), f32),
             pltpu.VMEM((4 * GROUPS, 3 * SPAN, FREQ, LANES), f32),
             pltpu.VMEM((4 * GROUPS, FREQ, LANES), f32),
             pltpu.VMEM((4 * GROUPS, 2, FREQ, LANES), f32),

time: 33.5 us -> 32.3 us (0.964)
  Pallas kernels: 32 us -> 30.6 us
    pallas_call x1, Pallas kernels: 29.9 us -> 28.4 us  [local(): pl.pallas_call(functools.partial(exchange_kernel, lon_size, lat_size), na...]
where the time goes in v4:
time: 32.3 us; the launch traced here: 31.9 us
  Pallas kernels  30.6 us (95%)
  between operations  1.3 us (4%)
    pallas_call x1, Pallas kernels, local(): pl.pallas_call(functools.partial(exchange_kernel, lon_size, lat_size), na...  28.4 us
    pallas_call x1, Pallas kernels, local(): pl.pallas_call(finish_kernel, name='finish', out_shape=(jax.ShapeDtypeStr...  2.15 us

profile of v4, /device:TPU:0, one launch (start us, length us, event | category | flops | bytes accessed | tf_op | source)
XLA Modules:
  0.0 31.9 jit_solution(8719948173443183553)
XLA Ops:
  1.3 0.0 copy-start
  1.3 28.4 %exchange.1 = (f32[5184,128]{1,0:T(8,128)S(1)}, f32[8,128]{1,0:T(8,128)S(1)}, f32[2,4,128]{2,1,0:T(4,128)S(1)}) custom-call(f32[36,36,4,1,128]{4,3,2,1,0:T(1,128)} %bitcast.7, f32[5184,128]{1,0:T(8,128)} %bitcast.8, s32[4,128]{1,0:T(4,128)} %sea_hbm.1, f32[2,4,128]{2,1,0:T(4,128)} %refr_hbm.1, f32[2,2,128]{2,1,0:T(2,128)} %atm_hbm.1, f32[1]{0:T(128)S(6)} %copy.13.hour, ...), custom_call_target="tpu_custom_call" | custom-call | tf_op jit(solution)/shard_map/exchange/pallas_call | solution.py:515
  29.7 0.0 copy-done
  29.7 2.2 %finish.1 = (f32[36,18,8,128]{3,2,1,0:T(8,128)}, f32[2,4,128]{2,1,0:T(4,128)}) custom-call(f32[36,18,8,128]{3,2,1,0:T(8,128)S(1)} %bitcast.6, f32[8,128]{1,0:T(8,128)S(1)} %get-tuple-element.8.energy, f32[2,4,128]{2,1,0:T(4,128)S(1)} %get-tuple-element.9.wind, f32[36]{0:T(128)S(1)} %copy-done), custom_call_target="tpu_custom_call" | custom-call | tf_op jit(solution)/shard_map/finish/pallas_call | solution.py:576
Async XLA Ops:
  1.3 28.4 %copy-start = (f32[36]{0:T(128)S(1)}, f32[36]{0:T(128)}, u32[]{:S(2)}) copy-start(f32[36]{0:T(128)} %constant.8.clone.decay) | copy-start | bytes 436

commit v5 on v4

--- a/solution.py
+++ b/solution.py
@@ -21,7 +21,7 @@
 CAP = 6
 BLOCKS = ((0, 8), (8, 8), (16, 8), (24, 8), (32, 4))
 FIRST = 2
-DEPTH = 12
+DEPTH = 9
 CLOSING = (DIRS - 2, DIRS - 1, 0)
 LAG = 5
 LOG2E = math.log2(math.e)
@@ -119,16 +119,6 @@
 
     barrier = pltpu.get_barrier_semaphore()
 
-    def greet(d, carry):
-        pl.semaphore_signal(
-            barrier, inc=1, device_id=(lax.rem(me + d, lon_size), la), device_id_type=MESH
-        )
-        return carry
-
-    lax.fori_loop(1, lon_size, greet, 0)
-    for peer in (north, south):
-        pl.semaphore_signal(barrier, inc=1, device_id=(me, peer), device_id_type=MESH)
-
     small = [
         (atm_hbm, atm),
         (cells_hbm, cells),
@@ -143,6 +133,16 @@
     ]
     for copy in small:
         copy.start()
+
+    def greet(d, carry):
+        pl.semaphore_signal(
+            barrier, inc=1, device_id=(lax.rem(me + d, lon_size), la), device_id_type=MESH
+        )
+        return carry
+
+    lax.fori_loop(1, lon_size, greet, 0)
+    for peer in (north, south):
+        pl.semaphore_signal(barrier, inc=1, device_id=(me, peer), device_id_type=MESH)
 
     whole = pltpu.make_async_copy(spec_rows, nat, x_sem)
     whole.start()

time: 32.3 us -> 32.3 us (level)
  no operation moved by 1% of the time
where the time goes in v5:
time: 32.3 us; the launch traced here: 31.9 us
  Pallas kernels  30.6 us (95%)
  between operations  1.3 us (4%)
    pallas_call x1, Pallas kernels, local(): pl.pallas_call(functools.partial(exchange_kernel, lon_size, lat_size), na...  28.4 us
    pallas_call x1, Pallas kernels, local(): pl.pallas_call(finish_kernel, name='finish', out_shape=(jax.ShapeDtypeStr...  2.15 us

profile of v5, /device:TPU:0, one launch (start us, length us, event | category | flops | bytes accessed | tf_op | source)
XLA Modules:
  0.0 31.9 jit_solution(7500859868521442023)
XLA Ops:
  1.3 0.0 copy-start
  1.3 28.4 %exchange.1 = (f32[5184,128]{1,0:T(8,128)S(1)}, f32[8,128]{1,0:T(8,128)S(1)}, f32[2,4,128]{2,1,0:T(4,128)S(1)}) custom-call(f32[36,36,4,1,128]{4,3,2,1,0:T(1,128)} %bitcast.7, f32[5184,128]{1,0:T(8,128)} %bitcast.8, s32[4,128]{1,0:T(4,128)} %sea_hbm.1, f32[2,4,128]{2,1,0:T(4,128)} %refr_hbm.1, f32[2,2,128]{2,1,0:T(2,128)} %atm_hbm.1, f32[1]{0:T(128)S(6)} %copy.13.hour, ...), custom_call_target="tpu_custom_call" | custom-call | tf_op jit(solution)/shard_map/exchange/pallas_call | solution.py:515
  29.7 0.0 copy-done
  29.7 2.2 %finish.1 = (f32[36,18,8,128]{3,2,1,0:T(8,128)}, f32[2,4,128]{2,1,0:T(4,128)}) custom-call(f32[36,18,8,128]{3,2,1,0:T(8,128)S(1)} %bitcast.6, f32[8,128]{1,0:T(8,128)S(1)} %get-tuple-element.8.energy, f32[2,4,128]{2,1,0:T(4,128)S(1)} %get-tuple-element.9.wind, f32[36]{0:T(128)S(1)} %copy-done), custom_call_target="tpu_custom_call" | custom-call | tf_op jit(solution)/shard_map/finish/pallas_call | solution.py:576
Async XLA Ops:
  1.3 28.4 %copy-start = (f32[36]{0:T(128)S(1)}, f32[36]{0:T(128)}, u32[]{:S(2)}) copy-start(f32[36]{0:T(128)} %constant.8.clone.decay) | copy-start | bytes 436
